TPU v7x, 32 devices: a whole 2x2x4 slice. The times are simulated.
32 devices in a mesh: seq: 8 (over z, x), chan: 4 (over y, core).
Axes of the slice: x: 2, y: 2, z: 4, core: 2. Of those that a mesh axis runs over, the one named last changes fastest.
Arguments:
- q_proj: bfloat16 [4096, 1024], P('seq', 'chan'), may hold values from -6 to 6
- k_proj: bfloat16 [4096, 1024], P('seq', 'chan'), may hold values from -6 to 6
- v_proj: bfloat16 [4096, 1024], P('seq', 'chan'), may hold values from -6 to 6
- short_taps: float32 [3, 7, 1024], P(None, None, 'chan'), may hold values from -2 to 2
- medium_taps: float32 [128, 1024], P(None, 'chan'), may hold values from -0.5 to 0.5
- long_taps: float32 [4096, 1024], P('seq', 'chan'), may hold values from -0.09375 to 0.09375
- grad_out: bfloat16 [4096, 1024], P('seq', 'chan'), may hold values from -6 to 6
- stretch_grads: bfloat16 [1024, 1024], P(('seq', 'chan')), may hold values from -6 to 6
- positions: int32 [1024], replicated, may hold values from 0 to 4095, as said below
Outputs:
- y_out: bfloat16 [4096, 1024], P('seq', 'chan')
- grad_q: bfloat16 [4096, 1024], P('seq', 'chan')
- grad_k: bfloat16 [4096, 1024], P('seq', 'chan')
- grad_v: bfloat16 [4096, 1024], P('seq', 'chan')
- grad_long: float32 [4096, 1024], P('seq', 'chan')
Inputs may be any that keep to these rules, and one draw needn't show every extreme that they name: 1024 distinct byte positions in increasing order; position 0 and position 4095 are always among them.
All inputs are finite; a program needn't handle non-finite values.
Results may differ from a plain program's by a relative error of at most 0.001.
Values may be sent and summed in bfloat16 or wider, within the bound.
A program may use at most 128 MiB of HBM per device.

v0:
```python
import math

import jax
import jax.numpy as jnp
from jax import lax
from jax.sharding import PartitionSpec as P

SHORT = 7
MED = 128


highest = lax.Precision.HIGHEST


def from_behind(array, axis, by):
    count = lax.axis_size(axis)
    pairs = [(i, i + by) for i in range(count) if 0 <= i + by < count]
    return lax.ppermute(array, axis, pairs)


def depthwise(padded, kernel):
    return lax.conv_general_dilated(
        padded[None],
        kernel[:, None, :],
        (1,),
        "VALID",
        dimension_numbers=("NWC", "WIO", "NWC"),
        feature_group_count=padded.shape[1],
        precision=highest,
    )[0]


def causal(padded, taps):
    return depthwise(padded, taps[::-1])


def anticausal(padded, taps):
    return depthwise(padded, taps)


def regroup(stacked):
    return lax.all_to_all(stacked, "seq", split_axis=1, concat_axis=1, tiled=True)


def angles(numer, denom):
    return (numer % denom).astype(jnp.float32) * (2.0 * math.pi / denom)


def column_table(rows, count):
    piece_rows = rows // count
    block_ids = lax.broadcasted_iota(jnp.int32, (count, piece_rows), 0)
    inside = lax.broadcasted_iota(jnp.int32, (count, piece_rows), 1)
    global_cols = block_ids * piece_rows + inside
    freqs = jnp.arange(rows, dtype=jnp.int32)
    omega = angles(freqs[:, None, None] * global_cols[None], rows)
    return (jnp.cos(omega), jnp.sin(omega), global_cols)


def forward_spectra(signals, count, index):
    members, rows, width = signals.shape
    piece_rows = rows // count
    freq_span = 2 * count
    full_size = freq_span * rows
    arrived_a = regroup(signals.reshape(members, count, piece_rows, width))
    freqs = jnp.arange(freq_span, dtype=jnp.int32)
    sources = jnp.arange(count, dtype=jnp.int32)
    coarse = angles(freqs[:, None] * sources[None, :], freq_span)
    real_a = jnp.einsum("ka,mabc->mkbc", jnp.cos(coarse), arrived_a, precision=highest)
    imag_a = -jnp.einsum("ka,mabc->mkbc", jnp.sin(coarse), arrived_a, precision=highest)
    global_b = index * piece_rows + jnp.arange(piece_rows, dtype=jnp.int32)
    phase = angles(freqs[:, None] * global_b[None, :], full_size)[None, :, :, None]
    cos_twist = jnp.cos(phase)
    sin_twist = jnp.sin(phase)
    real_t = real_a * cos_twist + imag_a * sin_twist
    imag_t = imag_a * cos_twist - real_a * sin_twist
    arrived_b = regroup(jnp.concatenate([real_t, imag_t], 0)).reshape(
        2 * members, count, 2, piece_rows, width
    )
    cos_b, sin_b, _ = column_table(rows, count)
    real_in = arrived_b[:members]
    imag_in = arrived_b[members:]
    spec_real = jnp.einsum("kjb,mjlbc->mlkc", cos_b, real_in, precision=highest) + jnp.einsum(
        "kjb,mjlbc->mlkc", sin_b, imag_in, precision=highest
    )
    spec_imag = jnp.einsum("kjb,mjlbc->mlkc", cos_b, imag_in, precision=highest) - jnp.einsum(
        "kjb,mjlbc->mlkc", sin_b, real_in, precision=highest
    )
    return (spec_real, spec_imag)


def inverse_signals(spec_real, spec_imag, count, index):
    members = spec_real.shape[0]
    rows = spec_real.shape[2]
    width = spec_real.shape[3]
    piece_rows = rows // count
    freq_span = 2 * count
    full_size = freq_span * rows
    cos_b, sin_b, global_cols = column_table(rows, count)
    wave_real = jnp.einsum("kjb,mlkc->mjlbc", cos_b, spec_real, precision=highest) - jnp.einsum(
        "kjb,mlkc->mjlbc", sin_b, spec_imag, precision=highest
    )
    wave_imag = jnp.einsum("kjb,mlkc->mjlbc", cos_b, spec_imag, precision=highest) + jnp.einsum(
        "kjb,mlkc->mjlbc", sin_b, spec_real, precision=highest
    )
    local_freq = 2 * index + jnp.arange(2, dtype=jnp.int32)
    phase = angles(local_freq[None, :, None] * global_cols[:, None, :], full_size)[
        None, :, :, :, None
    ]
    cos_twist = jnp.cos(phase)
    sin_twist = jnp.sin(phase)
    real_t = wave_real * cos_twist - wave_imag * sin_twist
    imag_t = wave_real * sin_twist + wave_imag * cos_twist
    arrived = regroup(jnp.concatenate([real_t, imag_t], 0)).reshape(
        2 * members, freq_span, piece_rows, width
    )
    targets = jnp.arange(count, dtype=jnp.int32)
    freqs = jnp.arange(freq_span, dtype=jnp.int32)
    coarse = angles(targets[:, None] * freqs[None, :], freq_span)
    signal = (
        jnp.einsum("ak,mkbc->mabc", jnp.cos(coarse), arrived[:members], precision=highest)
        - jnp.einsum("ak,mkbc->mabc", jnp.sin(coarse), arrived[members:], precision=highest)
    ) / full_size
    return regroup(signal).reshape(members, rows, width)


def times_conj(left_real, left_imag, right_real, right_imag):
    return (
        left_real * right_real + left_imag * right_imag,
        left_real * right_imag - left_imag * right_real,
    )


def local(
    q_proj, k_proj, v_proj, short_taps, medium_taps, long_taps, grad_out, stretch_grads, positions
):
    rows, width = q_proj.shape
    count = lax.axis_size("seq")
    index = lax.axis_index("seq")
    short_lead = SHORT - 1
    reach_rows = MED + SHORT - 2
    prev_q, prev_k, prev_v = from_behind(
        (q_proj[rows - short_lead :], k_proj[rows - short_lead :], v_proj[rows - reach_rows :]),
        "seq",
        1,
    )
    q_short = causal(jnp.concatenate([prev_q, q_proj], 0).astype(jnp.float32), short_taps[0])
    k_short = causal(jnp.concatenate([prev_k, k_proj], 0).astype(jnp.float32), short_taps[1])
    v_wide = causal(jnp.concatenate([prev_v, v_proj], 0).astype(jnp.float32), short_taps[2])
    middle = causal(v_wide, medium_taps)
    inner = k_short * middle
    column = lax.axis_index("chan") * width
    piece = lax.dynamic_slice_in_dim(
        lax.all_gather(stretch_grads, ("seq", "chan"), axis=0, tiled=True), column, width, 1
    )
    located = positions - index * rows
    onehot = (
        lax.broadcasted_iota(jnp.int32, (rows, piece.shape[0]), 0) == located[None, :]
    ).astype(jnp.bfloat16)
    placed = jnp.dot(onehot, piece, preferred_element_type=jnp.float32)
    out_grad = grad_out.astype(jnp.float32) + placed
    long_cot = out_grad * q_short
    fwd_real, fwd_imag = forward_spectra(jnp.stack([inner, long_taps]), count, index)
    prod_real = fwd_real[0] * fwd_real[1] - fwd_imag[0] * fwd_imag[1]
    prod_imag = fwd_real[0] * fwd_imag[1] + fwd_imag[0] * fwd_real[1]
    long_out = inverse_signals(prod_real[None], prod_imag[None], count, index)[0]
    cot_real, cot_imag = forward_spectra(long_cot[None], count, index)
    back_real, back_imag = times_conj(fwd_real[1], fwd_imag[1], cot_real[0], cot_imag[0])
    filt_real, filt_imag = times_conj(fwd_real[0], fwd_imag[0], cot_real[0], cot_imag[0])
    results = inverse_signals(
        jnp.stack([back_real, filt_real]), jnp.stack([back_imag, filt_imag]), count, index
    )
    inner_grad = results[0]
    long_grad = results[1]
    y_out = (q_short * long_out).astype(jnp.bfloat16)
    q_back = out_grad * long_out
    k_back = inner_grad * middle
    mid_back = inner_grad * k_short
    next_q, next_k, next_mid = from_behind(
        (q_back[:short_lead], k_back[:short_lead], mid_back[:reach_rows]), "seq", -1
    )
    v_back = anticausal(jnp.concatenate([mid_back, next_mid], 0), medium_taps)
    grad_q = anticausal(jnp.concatenate([q_back, next_q], 0), short_taps[0]).astype(jnp.bfloat16)
    grad_k = anticausal(jnp.concatenate([k_back, next_k], 0), short_taps[1]).astype(jnp.bfloat16)
    grad_v = anticausal(v_back, short_taps[2]).astype(jnp.bfloat16)
    grad_long = long_grad * (rows * count) ** (-0.5)
    return (y_out, grad_q, grad_k, grad_v, grad_long)


def solution(mesh):
    return jax.shard_map(
        local,
        mesh=mesh,
        in_specs=(
            P("seq", "chan"),
            P("seq", "chan"),
            P("seq", "chan"),
            P(None, None, "chan"),
            P(None, "chan"),
            P("seq", "chan"),
            P("seq", "chan"),
            P(("seq", "chan"), None),
            P(),
        ),
        out_specs=(
            P("seq", "chan"),
            P("seq", "chan"),
            P("seq", "chan"),
            P("seq", "chan"),
            P("seq", "chan"),
        ),
        check_vma=False,
    )
```

profile of v0, /device:TPU:0, one launch (start us, length us, event | category | flops | bytes accessed | tf_op | source)
XLA Modules:
  0.0 564.5 jit_solution(6718035227965905126)
XLA Ops:
  29.4 40.4 %all-gather.2.cloned.1.call-done = bf16[1024,1024]{1,0:T(8,128)(2,1)} async-done(((bf16[32,1024]{1,0:T(8,128)(2,1)}), bf16[1024,1024]{1,0:T(8,128)(2,1)}) %all-gather.2.cloned.1.call-update) | async-done | bytes 2097168 | tf_op jit(solution)/shard_map/all_gather | solution.py:153
  76.7 7.2 %fusion.158 = f32[1,512,256]{2,0,1:T(1,128)S(1)} fusion(f32[1,648,256]{2,0,1:T(1,128)S(1)} %reshape.266, f32[128,1,256]{2,0,1:T(8,128)S(1)} %bitcast.357), kind=kOutput, calls=%fused_computation.193 | convolution fusion | flops 201326592 | bytes 1318912 | tf_op jit(solution)/shard_map/conv_general_dilated | solution.py:22
  101.0 20.1 %all-to-all-done = f32[2,8,64,256]{3,2,0,1:T(8,128)S(1)} async-done(((f32[2,8,64,256]{3,2,0,1:T(8,128)}), f32[2,8,64,256]{3,2,0,1:T(8,128)S(1)}, u32[]{:S(2)}, u32[]{:S(2)}) %all-to-all-start) | async-done | bytes 1048608 | tf_op jit(solution)/shard_map/all_to_all | solution.py:42
  135.0 38.3 %all-to-all-done.5 = f32[2,16,64,256]{3,2,0,1:T(8,128)S(1)} async-done(((f32[2,16,64,256]{3,2,0,1:T(8,128)}), f32[2,16,64,256]{3,2,0,1:T(8,128)S(1)}, u32[]{:S(2)}, u32[]{:S(2)}) %all-to-all-start.5) | async-done | bytes 2097184 | tf_op jit(solution)/shard_map/all_to_all | solution.py:42
  178.5 5.9 %convolution_bitcast_fusion.3 = f32[2,256,512]{2,1,0:T(8,128)S(1)} fusion(f32[8,2,64,256]{3,2,1,0:T(8,128)S(1)} %bitcast.350, s32[8,64]{1,0:T(8,128)S(1)} %iota_add_fusion), kind=kOutput, calls=%fused_computation.53 | convolution fusion | flops 1614282752 | bytes 2099200 | tf_op jit(solution)/shard_map/kjb,mjlbc->mlkc/dot_general | solution.py:82
  184.4 7.3 %convolution_bitcast_fusion.1 = f32[2,256,512]{2,1,0:T(8,128)} fusion(f32[8,2,64,256]{3,2,1,0:T(8,128)S(1)} %bitcast.352, s32[8,64]{1,0:T(8,128)S(1)} %iota_add_fusion), kind=kOutput, calls=%fused_computation.51 | convolution fusion | flops 1614282752 | bytes 2099200 | tf_op jit(solution)/shard_map/kjb,mjlbc->mlkc/dot_general | solution.py:85
  191.7 6.8 %fusion.42 = f32[1,2,512,256]{2,3,1,0:T(8,128)} fusion(f32[2,256,512]{2,1,0:T(8,128)S(1)} %convolution_bitcast_fusion.3, f32[8,2,64,256]{3,2,1,0:T(8,128)S(1)} %bitcast.353, s32[8,64]{1,0:T(8,128)S(1)} %iota_add_fusion), kind=kOutput, calls=%fused_computation.60 | convolution fusion | flops 1614544896 | bytes 3147776 | tf_op jit(solution)/shard_map/kjb,mjlbc->mlkc/dot_general | solution.py:82
  198.5 71.9 %all-to-all-done.1 = f32[4,16,64,256]{3,2,0,1:T(8,128)} async-done(((f32[4,16,64,256]{3,2,0,1:T(8,128)}), f32[4,16,64,256]{3,2,0,1:T(8,128)}, u32[]{:S(2)}, u32[]{:S(2)}) %all-to-all-start.1) | async-done | bytes 4194336 | tf_op jit(solution)/shard_map/all_to_all | solution.py:42
  273.0 7.6 %fusion.11 = f32[2,2,256,512,1]{3,2,4,1,0:T(8,128)S(1)} fusion(f32[2,8,2,64,256]{4,3,0,2,1:T(8,128)S(1)} %bitcast.348, s32[8,64]{1,0:T(8,128)S(1)} %iota_add_fusion), kind=kOutput, calls=%fused_computation.28 | convolution fusion | flops 3224895488 | bytes 4196352 | tf_op jit(solution)/shard_map/kjb,mjlbc->mlkc/dot_general | solution.py:85
  280.6 7.5 %fusion.13 = f32[2,2,256,512,1]{3,2,4,1,0:T(8,128)S(1)} fusion(f32[2,8,2,64,256]{4,3,0,2,1:T(8,128)S(1)} %bitcast.349, s32[8,64]{1,0:T(8,128)S(1)} %iota_add_fusion), kind=kOutput, calls=%fused_computation.30 | convolution fusion | flops 3224895488 | bytes 4196352 | tf_op jit(solution)/shard_map/kjb,mjlbc->mlkc/dot_general | solution.py:82
  288.1 7.9 %fusion.2 = f32[2,2,512,256]{2,3,1,0:T(8,128)S(1)} fusion(f32[2,2,256,512,1]{3,2,4,1,0:T(8,128)S(1)} %fusion.11, f32[2,8,2,64,256]{4,3,0,2,1:T(8,128)S(1)} %bitcast.346, s32[8,64]{1,0:T(8,128)S(1)} %iota_add_fusion), kind=kOutput, calls=%fused_computation.13 | convolution fusion | flops 3225419776 | bytes 6293504 | tf_op jit(solution)/shard_map/kjb,mjlbc->mlkc/dot_general | solution.py:85
  296.0 7.7 %fusion.3 = f32[2,2,512,256]{2,3,1,0:T(8,128)S(1)} fusion(f32[2,2,256,512,1]{3,2,4,1,0:T(8,128)S(1)} %fusion.13, f32[2,8,2,64,256]{4,3,0,2,1:T(8,128)S(1)} %bitcast.347, s32[8,64]{1,0:T(8,128)S(1)} %iota_add_fusion), kind=kOutput, calls=%fused_computation.15 | convolution fusion | flops 3225419776 | bytes 6293504 | tf_op jit(solution)/shard_map/kjb,mjlbc->mlkc/dot_general | solution.py:82
  303.7 9.2 %multiply_add_fusion.1 = (f32[1,2,512,256]{2,3,1,0:T(8,128)}, f32[1,2,512,256]{2,3,1,0:T(8,128)}, f32[1,2,512,256]{2,3,1,0:T(8,128)}, f32[1,2,512,256]{2,3,1,0:T...) fusion(f32[1,2,512,256]{2,3,1,0:T(8,128)S(1)} %copy-done.20, ...), kind=kOutput, calls=%fused_computation.108 | convolution fusion | flops 1619263488 | bytes 13633536 | tf_op jit(solution)/shard_map/kjb,mjlbc->mlkc/dot_general | solution.py:85
  318.6 5.7 %fusion.57 = f32[2,256,8,64]{1,3,2,0:T(8,128)S(1)} fusion(f32[1,2,512,256]{2,3,1,0:T(8,128)S(1)} %get-tuple-element.15, s32[8,64]{1,0:T(8,128)S(1)} %iota_add_fusion), kind=kOutput, calls=%fused_computation.83 | convolution fusion | flops 1614282752 | bytes 2099200 | tf_op jit(solution)/shard_map/kjb,mlkc->mjlbc/dot_general | solution.py:102
  324.4 6.2 %fusion.40 = f32[1,8,2,64,256]{4,3,1,2,0:T(8,128)S(1)} fusion(f32[2,256,8,64]{1,3,2,0:T(8,128)S(1)} %fusion.55, f32[1,2,512,256]{2,3,1,0:T(8,128)S(1)} %get-tuple-element.15, s32[8,64]{1,0:T(8,128)S(1)} %iota_add_fusion), kind=kOutput, calls=%fused_computation.58 | convolution fusion | flops 1614544896 | bytes 3147776 | tf_op jit(solution)/shard_map/kjb,mlkc->mjlbc/dot_general | solution.py:99
  330.5 5.9 %multiply_subtract_fusion.3 = (f32[1,8,2,64,256]{4,3,1,2,0:T(8,128)S(1)}, f32[1,8,2,64,256]{4,3,1,2,0:T(8,128)S(1)}) fusion(f32[1,8,2,64,256]{4,3,1,2,0:T(8,128)S(1)} %fusion.40, f32[8,2,64]{2,0,1:T(8,128)S(1)} %get-tuple-element.38, f32[8,2,64]{2,0,1:T(8,128)S(1)} %get-tuple-element.37, f32[2,256,8,64]{1,3,2,0:T(8,128)S(1)} %fusion.57, ...), kind=kOutput, calls=%fused_computation.113 | convolution fusion | flops 1616117760 | bytes 5253120 | tf_op jit(solution)/shard_map/kjb,mlkc->mjlbc/dot_general | solution.py:102
  342.1 8.8 %fusion.20 = f32[2,2,256,8,64]{2,4,3,1,0:T(8,128)S(1)} fusion(f32[1,2,512,256]{2,3,1,0:T(8,128)S(1)} %copy-done.16, f32[1,2,512,256]{2,3,1,0:T(8,128)} %get-tuple-element.7, s32[8,64]{1,0:T(8,128)S(1)} %iota_add_fusion), kind=kOutput, calls=%fused_computation.37 | convolution fusion | flops 3225419776 | bytes 4196352 | tf_op jit(solution)/shard_map/kjb,mlkc->mjlbc/dot_general | solution.py:99
  351.0 7.6 %fusion.19 = f32[2,2,256,8,64]{2,4,3,1,0:T(8,128)S(1)} fusion(f32[1,2,512,256]{2,3,1,0:T(8,128)S(1)} %copy-done.17, f32[1,2,512,256]{2,3,1,0:T(8,128)S(1)} %copy-done.18, s32[8,64]{1,0:T(8,128)S(1)} %iota_add_fusion), kind=kOutput, calls=%fused_computation.36 | convolution fusion | flops 3225419776 | bytes 4196352 | tf_op jit(solution)/shard_map/kjb,mlkc->mjlbc/dot_general | solution.py:102
  358.6 7.5 %fusion.23 = f32[2,2,256,8,64]{2,4,3,1,0:T(8,128)S(1)} fusion(f32[2,2,256,8,64]{2,4,3,1,0:T(8,128)S(1)} %fusion.20, f32[1,2,512,256]{2,3,1,0:T(8,128)S(1)} %copy-done.15, f32[1,2,512,256]{2,3,1,0:T(8,128)S(1)} %copy-done.14, s32[8,64]{1,0:T(8,128)S(1)} %iota_add_fusion), kind=kOutput, calls=%fused_computation.40 | convolution fusion | flops 3225944064 | bytes 6293504 | tf_op jit(solution)/shard_map/kjb,mlkc->mjlbc/dot_general | solution.py:99
  366.1 8.3 %fusion = (f32[2,8,2,64,256]{4,3,1,2,0:T(8,128)S(1)}, f32[2,8,2,64,256]{4,3,1,2,0:T(8,128)S(1)}) fusion(f32[2,2,256,8,64]{2,4,3,1,0:T(8,128)S(1)} %fusion.23, f32[8,2,64]{2,0,1:T(8,128)S(1)} %get-tuple-element.38, f32[8,2,64]{2,0,1:T(8,128)S(1)} %get-tuple-element.37, f32[2,2,256,8,64]{2,4,3,1,0:T(8,128)S(1)} %fusion.19, s32[8,64]{1,0:T(8,128)S(1)} %iota_add_fusion, ...), kind=kOutput, calls=%fused_computation.8 | convolution fusion | flops 3229089792 | bytes 10496000 | tf_op jit(solution)/shard_map/kjb,mlkc->mjlbc/dot_general | solution.py:102
  377.2 13.2 %all-to-all-done.2 = f32[2,8,2,64,256]{4,3,2,0,1:T(8,128)S(1)} async-done(((f32[2,8,2,64,256]{4,3,2,0,1:T(8,128)}), f32[2,8,2,64,256]{4,3,2,0,1:T(8,128)S(1)}, u32[]{:S(2)}, u32[]{:S(2)}) %all-to-all-start.2) | async-done | bytes 2097184 | tf_op jit(solution)/shard_map/all_to_all | solution.py:42
  398.6 88.9 %all-to-all-done.6 = f32[4,8,2,64,256]{4,3,2,0,1:T(8,128)} async-done(((f32[4,8,2,64,256]{4,3,2,0,1:T(8,128)}), f32[4,8,2,64,256]{4,3,2,0,1:T(8,128)}, u32[]{:S(2)}, u32[]{:S(2)}) %all-to-all-start.6) | async-done | bytes 4194336 | tf_op jit(solution)/shard_map/all_to_all | solution.py:42
  518.2 17.4 %all-to-all-done.7 = f32[2,8,64,256]{3,2,0,1:T(8,128)S(1)} async-done(((f32[2,8,64,256]{3,2,0,1:T(8,128)}), f32[2,8,64,256]{3,2,0,1:T(8,128)S(1)}, u32[]{:S(2)}, u32[]{:S(2)}) %all-to-all-start.7) | async-done | bytes 1048608 | tf_op jit(solution)/shard_map/all_to_all | solution.py:42
  544.9 10.8 %fusion.88 = f32[1,518,256]{2,0,1:T(1,128)S(1)} fusion(f32[1,645,256]{2,1,0:T(8,128)S(1)} %maximum_bitcast_fusion.10, f32[128,1,256]{2,0,1:T(8,128)S(1)} %bitcast.356), kind=kOutput, calls=%fused_computation.126 | convolution fusion | flops 203685888 | bytes 1321984 | tf_op jit(solution)/shard_map/conv_general_dilated | solution.py:22
  (166 shorter events, 131.2 us)
Async XLA Ops:
  7.2 18.6 %copy-start.9 = (bf16[512,256]{1,0:T(8,128)(2,1)S(1)}, bf16[512,256]{1,0:T(8,128)(2,1)}, u32[]{:S(2)}) copy-start(bf16[512,256]{1,0:T(8,128)(2,1)} %param.10) | copy-start | bytes 786436
  7.2 62.7 %all-gather.2.cloned.1.call-start = ((), (), s32[]{:S(2)}) async-start(), calls=%async_computation.8 | async-start | bytes 2162688 | tf_op jit(solution)/shard_map/all_gather | solution.py:153
  8.6 15.9 %collective-permute-start = (bf16[6,256]{1,0:T(8,128)(2,1)S(1)}, bf16[6,256]{1,0:T(8,128)(2,1)S(1)}, u32[]{:S(2)}, u32[]{:S(2)}) collective-permute-start(bf16[6,256]{1,0:T(8,128)(2,1)S(1)} %slice.98), channel_id=1, source_target_pairs={{0,4},{4,8},{8,12},{12,16},{16,20},{20,24},{24,28},{1,5},{5,9},{9,... | collective-permute-start | bytes 9224 | tf_op jit(solution)/shard_map/ppermute | solution.py:18
  14.2 11.6 %collective-permute-start.1 = (bf16[6,256]{1,0:T(8,128)(2,1)S(1)}, bf16[6,256]{1,0:T(8,128)(2,1)S(1)}, u32[]{:S(2)}, u32[]{:S(2)}) collective-permute-start(bf16[6,256]{1,0:T(8,128)(2,1)S(1)} %slice.100), channel_id=1, source_target_pairs={{0,4},{4,8},{8,12},{12,16},{16,20},{20,24},{24,28},{1,5},{5,9},{9,... | collective-permute-start | bytes 9224 | tf_op jit(solution)/shard_map/ppermute | solution.py:18
  18.5 8.9 %collective-permute-start.2 = (bf16[133,256]{1,0:T(8,128)(2,1)S(1)}, bf16[133,256]{1,0:T(8,128)(2,1)S(1)}, u32[]{:S(2)}, u32[]{:S(2)}) collective-permute-start(bf16[133,256]{1,0:T(8,128)(2,1)S(1)} %slice.102), channel_id=1, source_target_pairs={{0,4},{4,8},{8,12},{12,16},{16,20},{20,24},{24,28},{1,5},{5,9},{9,... | collective-permute-start | bytes 204296 | tf_op jit(solution)/shard_map/ppermute | solution.py:18
  27.1 42.7 %copy-start.2 = (f32[1,520,256]{2,1,0:T(8,128)}, f32[1,520,256]{2,1,0:T(8,128)S(1)}, u32[]{:S(2)}) copy-start(f32[1,520,256]{2,1,0:T(8,128)S(1)} %reshape.184) | copy-start | bytes 1597444
  27.4 56.5 %copy-start = (f32[1,520,256]{2,1,0:T(8,128)}, f32[1,520,256]{2,1,0:T(8,128)S(1)}, u32[]{:S(2)}) copy-start(f32[1,520,256]{2,1,0:T(8,128)S(1)} %reshape.191) | copy-start | bytes 1597444
  28.5 41.4 %copy-start.10 = (bf16[512,256]{1,0:T(8,128)(2,1)S(1)}, bf16[512,256]{1,0:T(8,128)(2,1)}, u32[]{:S(2)}) copy-start(bf16[512,256]{1,0:T(8,128)(2,1)} %param.15) | copy-start | bytes 786436
  72.3 19.2 %all-to-all-start.4 = ((f32[1,8,64,256]{3,2,0,1:T(8,128)}), f32[1,8,64,256]{3,2,0,1:T(8,128)S(1)}, u32[]{:S(2)}, u32[]{:S(2)}) async-start(f32[1,8,64,256]{3,2,0,1:T(8,128)} %bitcast.63), calls=%async_computation.4 | async-start | bytes 1048576 | tf_op jit(solution)/shard_map/all_to_all | solution.py:42
  91.5 29.6 %all-to-all-start = ((f32[2,8,64,256]{3,2,0,1:T(8,128)}), f32[2,8,64,256]{3,2,0,1:T(8,128)S(1)}, u32[]{:S(2)}, u32[]{:S(2)}) async-start(f32[2,8,64,256]{3,2,0,1:T(8,128)} %copy.183), calls=%async_computation | async-start | bytes 2097152 | tf_op jit(solution)/shard_map/all_to_all | solution.py:42
  121.1 52.2 %all-to-all-start.5 = ((f32[2,16,64,256]{3,2,0,1:T(8,128)}), f32[2,16,64,256]{3,2,0,1:T(8,128)S(1)}, u32[]{:S(2)}, u32[]{:S(2)}) async-start(f32[2,16,64,256]{3,2,0,1:T(8,128)} %copy.208), calls=%async_computation.5 | async-start | bytes 4194304 | tf_op jit(solution)/shard_map/all_to_all | solution.py:42
  173.3 97.1 %all-to-all-start.1 = ((f32[4,16,64,256]{3,2,0,1:T(8,128)}), f32[4,16,64,256]{3,2,0,1:T(8,128)}, u32[]{:S(2)}, u32[]{:S(2)}) async-start(f32[4,16,64,256]{3,2,0,1:T(8,128)} %copy.186), calls=%async_computation.1 | async-start | bytes 8388608 | tf_op jit(solution)/shard_map/all_to_all | solution.py:42
  338.1 52.2 %all-to-all-start.2 = ((f32[2,8,2,64,256]{4,3,2,0,1:T(8,128)}), f32[2,8,2,64,256]{4,3,2,0,1:T(8,128)S(1)}, u32[]{:S(2)}, u32[]{:S(2)}) async-start(f32[2,8,2,64,256]{4,3,2,0,1:T(8,128)} %copy.197), calls=%async_computation.2 | async-start | bytes 4194304 | tf_op jit(solution)/shard_map/all_to_all | solution.py:42
  342.1 8.8 %copy-start.17 = (f32[1,2,512,256]{2,3,1,0:T(8,128)S(1)}, f32[1,2,512,256]{2,3,1,0:T(8,128)}, u32[]{:S(2)}) copy-start(f32[1,2,512,256]{2,3,1,0:T(8,128)} %get-tuple-element.6) | copy-start | bytes 3145732
  390.3 97.1 %all-to-all-start.6 = ((f32[4,8,2,64,256]{4,3,2,0,1:T(8,128)}), f32[4,8,2,64,256]{4,3,2,0,1:T(8,128)}, u32[]{:S(2)}, u32[]{:S(2)}) async-start(f32[4,8,2,64,256]{4,3,2,0,1:T(8,128)} %copy.219), calls=%async_computation.6 | async-start | bytes 8388608 | tf_op jit(solution)/shard_map/all_to_all | solution.py:42
  487.4 18.5 %all-to-all-start.3 = ((f32[1,8,64,256]{3,2,0,1:T(8,128)}), f32[1,8,64,256]{3,2,0,1:T(8,128)S(1)}, u32[]{:S(2)}, u32[]{:S(2)}) async-start(f32[1,8,64,256]{3,2,0,1:T(8,128)} %copy.202), calls=%async_computation.3 | async-start | bytes 1048576 | tf_op jit(solution)/shard_map/all_to_all | solution.py:42
  498.9 10.6 %copy-start.3 = (f32[1,520,256]{2,1,0:T(8,128)S(1)}, f32[1,520,256]{2,1,0:T(8,128)}, u32[]{:S(2)}) copy-start(f32[1,520,256]{2,1,0:T(8,128)} %copy-done.2) | copy-start | bytes 1597444
  498.9 10.6 %copy-start.6 = (f32[512,256]{1,0:T(8,128)S(1)}, f32[512,256]{1,0:T(8,128)}, u32[]{:S(2)}) copy-start(f32[512,256]{1,0:T(8,128)} %get-tuple-element.42) | copy-start | bytes 1572868
  505.9 29.7 %all-to-all-start.7 = ((f32[2,8,64,256]{3,2,0,1:T(8,128)}), f32[2,8,64,256]{3,2,0,1:T(8,128)S(1)}, u32[]{:S(2)}, u32[]{:S(2)}) async-start(f32[2,8,64,256]{3,2,0,1:T(8,128)} %copy.224), calls=%async_computation.7 | async-start | bytes 2097152 | tf_op jit(solution)/shard_map/all_to_all | solution.py:42
  510.4 5.9 %collective-permute-start.3 = (f32[6,256]{1,0:T(8,128)S(1)}, f32[6,256]{1,0:T(8,128)S(1)}, u32[]{:S(2)}, u32[]{:S(2)}) collective-permute-start(f32[6,256]{1,0:T(8,128)S(1)} %slice.150), channel_id=1, source_target_pairs={{4,0},{8,4},{12,8},{16,12},{20,16},{24,20},{28,24},{5,1},{9,5},{13... | collective-permute-start | bytes 18440 | tf_op jit(solution)/shard_map/ppermute | solution.py:18
  517.3 18.3 %copy-start.1 = (f32[1,520,256]{2,1,0:T(8,128)S(1)}, f32[1,520,256]{2,1,0:T(8,128)}, u32[]{:S(2)}) copy-start(f32[1,520,256]{2,1,0:T(8,128)} %copy-done) | copy-start | bytes 1597444
  517.3 18.3 %copy-start.5 = (f32[1,512,256]{2,0,1:T(1,128)S(1)}, f32[1,512,256]{2,0,1:T(1,128)}, u32[]{:S(2)}) copy-start(f32[1,512,256]{2,0,1:T(1,128)} %copy-done.4) | copy-start | bytes 1572868
  535.8 8.7 %collective-permute-start.5 = (f32[133,256]{1,0:T(8,128)S(1)}, f32[133,256]{1,0:T(8,128)S(1)}, u32[]{:S(2)}, u32[]{:S(2)}) collective-permute-start(f32[133,256]{1,0:T(8,128)S(1)} %slice.161), channel_id=1, source_target_pairs={{4,0},{8,4},{12,8},{16,12},{20,16},{24,20},{28,24},{5,1},{9,5},{13... | collective-permute-start | bytes 408584 | tf_op jit(solution)/shard_map/ppermute | solution.py:18
  537.1 6.2 %collective-permute-start.4 = (f32[6,256]{1,0:T(8,128)S(1)}, f32[6,256]{1,0:T(8,128)S(1)}, u32[]{:S(2)}, u32[]{:S(2)}) collective-permute-start(f32[6,256]{1,0:T(8,128)S(1)} %slice.158), channel_id=1, source_target_pairs={{4,0},{8,4},{12,8},{16,12},{20,16},{24,20},{28,24},{5,1},{9,5},{13... | collective-permute-start | bytes 18440 | tf_op jit(solution)/shard_map/ppermute | solution.py:18
  (12 other events, 55.7 us)
Sparse Core Ops, SparseCore 0:
  10.8 58.9 all-gather.1
where the time goes:
time: 575 us; the launch traced here: 564 us
  waiting for transfers between devices  311 us (54%)
  matrix products  153 us (27%)
  starting transfers between devices  48.1 us (8%)
  local copies, waits for them, and re-layouts  31.3 us (5%)
  between operations  15.3 us (3%)
    all_to_all x8, waiting for transfers between devices, regroup(): lax.all_to_all(stacked, 'seq', split_axis=1, concat_axis=1, tiled=True)  261 us
    all_gather x1, waiting for transfers between devices, local(): lax.all_gather(stretch_grads, ('seq', 'chan'), axis=0, tiled=True)  40.4 us
    all_to_all x8, starting transfers between devices, regroup(): lax.all_to_all(stacked, 'seq', split_axis=1, concat_axis=1, tiled=True)  32.5 us
    conv_general_dilated x8, matrix products, depthwise(): lax.conv_general_dilated(padded[None], kernel[:, None, :], (1,), 'VALID',...  19.8 us
    dot_general x2, matrix products, forward_spectra(): jnp.einsum('kjb,mjlbc->mlkc', cos_b, imag_in, precision=highest)  16.8 us
    ppermute x6, starting transfers between devices, from_behind(): return lax.ppermute(array, axis, pairs)  15.6 us
    dot_general x2, matrix products, forward_spectra(): jnp.einsum('kjb,mjlbc->mlkc', sin_b, real_in, precision=highest)  15.2 us
    dot_general x2, matrix products, inverse_signals(): jnp.einsum('kjb,mlkc->mjlbc', sin_b, spec_imag, precision=highest)  15 us
  transfers between devices with their start and end apart: 15, of which 11 were waited for; matrix products, arithmetic and copies ran while one was open for 19% of the time, Pallas kernels for 0%

commit v1 on v0

v1 whole, which is shorter than its diff:
```python
import functools
import math

import jax
import jax.numpy as jnp
import numpy as np
from jax import lax
from jax.experimental import pallas as pl
from jax.experimental.pallas import tpu as pltpu
from jax.sharding import PartitionSpec as P

SHORT = 7
MED = 128
LANES = 128
f32 = jnp.float32
bf16 = jnp.bfloat16


def fourier(rows):
    full = 2 * rows
    order = np.concatenate([np.arange(0, rows, 2), np.arange(1, rows, 2)])
    time = np.arange(rows)
    angle = ((time[:, None] * order[None, :]) % full) * (2.0 * math.pi / full)
    real, imag = np.cos(angle), -np.sin(angle)
    imag[:, 0] = 1.0 - 2.0 * (time % 2)
    table = jnp.asarray(np.concatenate([real, imag], 1), f32)
    return table


def halves(x):
    high = x.astype(bf16)
    return high, (x - high.astype(f32)).astype(bf16)


def product(left, right, dims):
    (lh, ll), (rh, rl) = left, right
    dot = functools.partial(
        lax.dot_general, dimension_numbers=(dims, ((), ())), preferred_element_type=f32
    )
    return dot(lh, rh) + (dot(lh, rl) + dot(ll, rh))


def pack_kernel(q_ref, k_ref, v_ref, g_ref, l_ref, out_ref):
    rows = q_ref.shape[0]
    for slot, ref in enumerate((q_ref, k_ref, v_ref, g_ref)):
        out_ref[:, slot * rows : (slot + 1) * rows] = ref[...].astype(f32).T.astype(bf16)
    high, low = halves(l_ref[...].T)
    out_ref[:, 4 * rows : 5 * rows] = high
    out_ref[:, 5 * rows : 6 * rows] = low


def unpack_kernel(in_ref, y_ref, gq_ref, gk_ref, gv_ref, gl_ref):
    rows = y_ref.shape[0]
    for slot, ref in enumerate((y_ref, gq_ref, gk_ref, gv_ref)):
        ref[...] = in_ref[:, slot * rows : (slot + 1) * rows].astype(f32).T.astype(bf16)
    total = in_ref[:, 4 * rows : 5 * rows].astype(f32) + in_ref[:, 5 * rows : 6 * rows].astype(f32)
    gl_ref[...] = total.T


def from_before(tail, width):
    lane = lax.broadcasted_iota(jnp.int32, tail.shape, 1)
    return jnp.where(lane >= width, pltpu.roll(tail, width, 1), 0.0)


def from_after(head, width):
    lanes = head.shape[1]
    lane = lax.broadcasted_iota(jnp.int32, head.shape, 1)
    return jnp.where(lane < lanes - width, pltpu.roll(head, lanes - width, 1), 0.0)


def put(ref, start, value):
    for h in range(value.shape[1] // LANES):
        ref[h, start : start + value.shape[0], :] = value[:, h * LANES : (h + 1) * LANES]


def get(ref, start, size):
    return jnp.concatenate([ref[h, start : start + size, :] for h in range(ref.shape[0])], 1)


def operator_kernel(
    scale,
    in_ref,
    s_ref,
    pos_ref,
    st_ref,
    mt_ref,
    fh_ref,
    fl_ref,
    out_ref,
    ext,
    wide,
    turned,
    qs,
    ks,
    mid,
    og,
    xs,
    ls,
    cs,
    us,
):
    lanes = in_ref.shape[0]
    rows = in_ref.shape[1] // 6
    tiles = lanes // LANES
    count, _, width, _ = xs.shape
    table = (fh_ref[...], fl_ref[...])

    def block(slot):
        return in_ref[:, slot * rows : (slot + 1) * rows]

    def short_causal(slot, which, out, start):
        value = block(slot).astype(f32).T
        put(ext, 8, value)
        put(ext, 0, from_before(value[rows - 8 :], width))
        for h in range(tiles):
            for r in range(0, rows, LANES):
                acc = jnp.zeros((LANES, LANES), f32)
                for j in range(SHORT):
                    tap = st_ref[h, which * 8 + j : which * 8 + j + 1, :]
                    acc = acc + tap * ext[h, r + 8 - j : r + 8 - j + LANES, :]
                out[h, start + r : start + r + LANES, :] = acc

    def short_anti(value, which, slot):
        put(ext, 0, value)
        put(ext, rows, from_after(value[:8], width))
        for h in range(tiles):
            for r in range(0, rows, LANES):
                acc = jnp.zeros((LANES, LANES), f32)
                for j in range(SHORT):
                    tap = st_ref[h, which * 8 + j : which * 8 + j + 1, :]
                    acc = acc + tap * ext[h, r + j : r + j + LANES, :]
                out_ref[
                    h * LANES : (h + 1) * LANES, slot * rows + r : slot * rows + r + LANES
                ] = acc.T.astype(bf16)

    def medium(out, back):
        size = rows + MED
        for s in range(8):
            for h in range(tiles):
                start = s if back else 8 - s
                turned[s, h, :, :] = wide[h, start : start + size, :]

        def step(n, carry):
            h = n // (rows // LANES)
            base = pl.multiple_of((n % (rows // LANES)) * LANES, LANES)
            acc = jnp.zeros((LANES, LANES), f32)
            for s in range(8):
                window = turned[s, h, pl.ds(base, LANES + MED), :]
                for m in range(MED // 8):
                    lead = 8 * m if back else MED - 8 * m
                    tap = mt_ref[h, 8 * m + s : 8 * m + s + 1, :]
                    acc = acc + tap * window[lead : lead + LANES]
            out[h, pl.ds(base, LANES), :] = acc
            return carry

        lax.fori_loop(0, tiles * (rows // LANES), step, 0)

    short_causal(0, 0, qs, 0)
    short_causal(1, 1, ks, 0)
    short_causal(2, 2, wide, MED + 8)
    put(wide, 8, from_before(get(wide, 8 + rows, MED), width))
    for h in range(tiles):
        wide[h, 0:8, :] = jnp.zeros((8, LANES), f32)
    medium(mid, False)

    stretches = pos_ref.shape[0]
    for a in range(count):
        spot = lax.broadcasted_iota(jnp.int32, (stretches, rows), 1) + a * rows
        onehot = (pos_ref[...] == spot).astype(f32).astype(bf16)
        placed = jnp.dot(s_ref[...], onehot, preferred_element_type=f32)
        piece = in_ref[a * width : (a + 1) * width, 3 * rows : 4 * rows].astype(f32) + placed
        us[a * width : (a + 1) * width, 0:rows] = piece
    put(og, 0, us[:, 0:rows].T)

    first = lax.broadcasted_iota(jnp.int32, (count, width, rows), 2) == 0

    def keep(ref, signal, masked):
        spectrum = product(signal, table, ((1,), (0,)))
        real = spectrum[:, :rows].reshape(count, width, rows)
        imag = spectrum[:, rows:].reshape(count, width, rows)
        ref[:, 0] = real
        ref[:, 1] = jnp.where(first, 0.0, imag) if masked else imag
        if masked:
            ref[:, 2] = jnp.where(first, imag, real)

    keep(ls, (block(4), block(5)), True)
    keep(xs, halves((get(ks, 0, rows) * get(mid, 0, rows)).T), True)
    keep(cs, halves((get(og, 0, rows) * get(qs, 0, rows)).T), False)

    lane = lax.broadcasted_iota(jnp.int32, (width, rows), 1)
    weight = jnp.where(lane == 0, 1.0, 2.0) / (2 * rows)
    sign = jnp.where(lane < rows // 2, 1.0, -1.0) * weight
    zero = jnp.zeros((width, rows), f32)

    def emit(i, now, before, factor):
        base = pl.multiple_of(i * width, width)
        us[pl.ds(base, width), 0:rows] = (now[0] * weight + before[0] * sign) * factor
        us[pl.ds(base, width), rows : 2 * rows] = (now[1] * weight + before[1] * sign) * factor

    def convolve():
        def outer(i, before):
            def inner(b, total):
                xr, lr, li, lq = xs[i - b, 0], ls[b, 0], ls[b, 1], ls[b, 2]
                masked = xs[i - b, 1]
                xi = jnp.where(lane == 0, xs[i - b, 2], masked)
                return (
                    total[0] + (xr * lr - xi * li),
                    total[1] + (xr * li + xi * lq),
                )

            now = lax.fori_loop(0, i + 1, inner, (zero, zero))
            emit(i, now, before, 1.0)
            return now

        lax.fori_loop(0, count, outer, (zero, zero))

    def correlate(ref, factor):
        def outer(n, before):
            d = count - 1 - n

            def inner(b, total):
                cr, ci = cs[b + d, 0], cs[b + d, 1]
                ar, ai, aq = ref[b, 0], ref[b, 1], ref[b, 2]
                return (
                    total[0] + (cr * ar + ci * ai),
                    total[1] + (ci * aq - cr * ai),
                )

            now = lax.fori_loop(0, n + 1, inner, (zero, zero))
            emit(d, now, before, factor)
            return now

        lax.fori_loop(0, count, outer, (zero, zero))

    correlate(xs, scale)
    high, low = halves(product(halves(us[...]), table, ((1,), (1,))))
    out_ref[:, 4 * rows : 5 * rows] = high
    out_ref[:, 5 * rows : 6 * rows] = low

    convolve()
    long_out = product(table, halves(us[...]), ((1,), (1,)))
    out_ref[:, 0:rows] = (get(qs, 0, rows) * long_out).T.astype(bf16)
    short_anti(get(og, 0, rows) * long_out, 0, 1)

    correlate(ls, 1.0)
    inner_grad = product(table, halves(us[...]), ((1,), (1,)))
    mid_back = inner_grad * get(ks, 0, rows)
    put(wide, 0, mid_back)
    put(wide, rows, from_after(mid_back[:MED], width))
    for h in range(tiles):
        wide[h, rows + MED : rows + MED + 8, :] = jnp.zeros((8, LANES), f32)
    short_anti(inner_grad * get(mid, 0, rows), 1, 2)
    medium(qs, True)
    short_anti(get(qs, 0, rows), 2, 3)


def whole_spec(n):
    return [pl.BlockSpec(memory_space=pltpu.VMEM)] * n


def local(
    q_proj, k_proj, v_proj, short_taps, medium_taps, long_taps, grad_out, stretch_grads, positions
):
    rows, lanes = q_proj.shape
    count = lax.axis_size("seq")
    index = lax.axis_index("seq")
    width = lanes // count
    tiles = lanes // LANES

    packed = pl.pallas_call(
        pack_kernel,
        out_shape=jax.ShapeDtypeStruct((lanes, 6 * rows), bf16),
        in_specs=whole_spec(5),
        out_specs=whole_spec(1)[0],
        name="pack",
    )(q_proj, k_proj, v_proj, grad_out, long_taps)

    mine = lax.all_to_all(stretch_grads, "chan", split_axis=1, concat_axis=0, tiled=True)
    mine = mine.T.reshape(count, width, mine.shape[0])
    stretch = lax.all_to_all(mine, "seq", split_axis=0, concat_axis=0, tiled=True)
    stretch = stretch.transpose(1, 0, 2).reshape(width, -1)

    arrived = lax.all_to_all(
        packed.reshape(count, width, 6 * rows), "seq", split_axis=0, concat_axis=0, tiled=True
    ).reshape(lanes, 6 * rows)

    def spread(taps):
        part = lax.dynamic_slice_in_dim(taps, index * width, width, 1)
        part = jnp.tile(part, (1, count))
        return part.reshape(taps.shape[0], tiles, LANES).transpose(1, 0, 2)

    short = spread(jnp.pad(short_taps, ((0, 0), (0, 1), (0, 0))).reshape(24, lanes))
    medium = spread(medium_taps)
    table = fourier(rows)
    fh, fl = halves(table)
    scratch = [
        pltpu.VMEM((tiles, rows + 8, LANES), f32),
        pltpu.VMEM((tiles, rows + MED + 8, LANES), f32),
        pltpu.VMEM((8, tiles, rows + MED, LANES), f32),
        pltpu.VMEM((tiles, rows, LANES), f32),
        pltpu.VMEM((tiles, rows, LANES), f32),
        pltpu.VMEM((tiles, rows, LANES), f32),
        pltpu.VMEM((tiles, rows, LANES), f32),
        pltpu.VMEM((count, 3, width, rows), f32),
        pltpu.VMEM((count, 3, width, rows), f32),
        pltpu.VMEM((count, 2, width, rows), f32),
        pltpu.VMEM((lanes, 2 * rows), f32),
    ]
    result = pl.pallas_call(
        functools.partial(operator_kernel, (rows * count) ** (-0.5)),
        out_shape=jax.ShapeDtypeStruct((lanes, 6 * rows), bf16),
        in_specs=whole_spec(7),
        out_specs=whole_spec(1)[0],
        scratch_shapes=scratch,
        name="operator",
    )(arrived, stretch, positions[:, None], short, medium, fh, fl)

    back = lax.all_to_all(
        result.reshape(count, width, 6 * rows), "seq", split_axis=0, concat_axis=0, tiled=True
    ).reshape(lanes, 6 * rows)
    return pl.pallas_call(
        unpack_kernel,
        out_shape=[jax.ShapeDtypeStruct((rows, lanes), bf16)] * 4
        + [jax.ShapeDtypeStruct((rows, lanes), f32)],
        in_specs=whole_spec(1),
        out_specs=whole_spec(5),
        name="unpack",
    )(back)


def solution(mesh):
    return jax.shard_map(
        local,
        mesh=mesh,
        in_specs=(
            P("seq", "chan"),
            P("seq", "chan"),
            P("seq", "chan"),
            P(None, None, "chan"),
            P(None, "chan"),
            P("seq", "chan"),
            P("seq", "chan"),
            P(("seq", "chan"), None),
            P(),
        ),
        out_specs=(
            P("seq", "chan"),
            P("seq", "chan"),
            P("seq", "chan"),
            P("seq", "chan"),
            P("seq", "chan"),
        ),
        check_vma=False,
    )
```

time: 575 us -> 142 us (0.25); the launches traced: 564 us -> 142 us
  waiting for transfers between devices: 311 us -> 36.3 us
  matrix products: 153 us -> 0 us
  blocking collectives: 0 us -> 48.9 us
  Pallas kernels: 0 us -> 40.2 us
  starting transfers between devices: 48.1 us -> 9.52 us
  local copies, waits for them, and re-layouts: 31.3 us -> 6.16 us
  between operations: 15.3 us -> 0.7 us
    all_to_all x8 -> x2, waiting for transfers between devices: 261 us -> 36.3 us  [the longest x1 32.3 us: local(): lax.all_to_all(packed.reshape(count, width, 6 * rows), 'seq', split_axis=...]
    dot_general x25 -> x0, matrix products: 133 us -> none  [the longest x2 16.8 us: forward_spectra(): jnp.einsum('kjb,mjlbc->mlkc', cos_b, imag_in, precision=highest)]
    all_to_all x0 -> x2, blocking collectives: none -> 48.9 us  [the longest x1 40.7 us: local(): lax.all_to_all(result.reshape(count, width, 6 * rows), 'seq', split_axis=...]
    all_gather x1 -> x0, waiting for transfers between devices: 40.4 us -> none  [local(): lax.all_gather(stretch_grads, ('seq', 'chan'), axis=0, tiled=True)]
    pallas_call x0 -> x3, Pallas kernels: none -> 40.2 us  [the longest x1 34.5 us: local(): pl.pallas_call(functools.partial(operator_kernel, (rows * count) ** (-0.5...]
    all_to_all x8 -> x2, starting transfers between devices: 32.5 us -> 9.52 us  [the longest x1 5.81 us: local(): lax.all_to_all(mine, 'seq', split_axis=0, concat_axis=0, tiled=True)]
    conv_general_dilated x8 -> x0, matrix products: 19.8 us -> none  [depthwise(): lax.conv_general_dilated(padded[None], kernel[:, None, :], (1,), 'VALID',...]
    ppermute x6 -> x0, starting transfers between devices: 15.6 us -> none  [from_behind(): return lax.ppermute(array, axis, pairs)]
  transfers between devices with their start and end apart: 15 -> 2, of which waited for: 11 -> 2; matrix products, arithmetic and copies ran while one was open for 19% -> 2% of each run, Pallas kernels for 0% -> 2%
where the time goes in v1:
time: 142 us
  blocking collectives  48.9 us (34%)
  Pallas kernels  40.2 us (28%)
  waiting for transfers between devices  36.3 us (26%)
  starting transfers between devices  9.52 us (7%)
  local copies, waits for them, and re-layouts  6.16 us (4%)
    all_to_all x1, blocking collectives, local(): lax.all_to_all(result.reshape(count, width, 6 * rows), 'seq', split_axis=...  40.7 us
    pallas_call x1, Pallas kernels, local(): pl.pallas_call(functools.partial(operator_kernel, (rows * count) ** (-0.5...  34.5 us
    all_to_all x1, waiting for transfers between devices, local(): lax.all_to_all(packed.reshape(count, width, 6 * rows), 'seq', split_axis=...  32.3 us
    all_to_all x1, blocking collectives, local(): lax.all_to_all(stretch_grads, 'chan', split_axis=1, concat_axis=0, tiled=...  8.17 us
    all_to_all x1, starting transfers between devices, local(): lax.all_to_all(mine, 'seq', split_axis=0, concat_axis=0, tiled=True)  5.81 us
    all_to_all x1, waiting for transfers between devices, local(): lax.all_to_all(mine, 'seq', split_axis=0, concat_axis=0, tiled=True)  3.92 us
    all_to_all x1, starting transfers between devices, local(): lax.all_to_all(packed.reshape(count, width, 6 * rows), 'seq', split_axis=...  3.71 us
    pallas_call x1, Pallas kernels, local(): pl.pallas_call(pack_kernel, out_shape=jax.ShapeDtypeStruct((lanes, 6 * ro...  2.98 us
  transfers between devices with their start and end apart: 2, of which 2 were waited for; matrix products, arithmetic and copies ran while one was open for 2% of the time, Pallas kernels for 2%

profile of v1, /device:TPU:0, one launch (start us, length us, event | category | flops | bytes accessed | tf_op | source)
XLA Modules:
  0.0 141.7 jit_solution(6710165427402443595)
XLA Ops:
  0.6 0.0 copy-start
  0.6 0.9 copy.40
  1.5 8.2 %all_to_all.34 = bf16[32,4,256]{2,0,1:T(8,128)(2,1)S(1)} all-to-all(bf16[32,4,256]{2,0,1:T(8,128)(2,1)S(1)} %bitcast.35), channel_id=1, replica_groups=mesh['seq'=8,'chan'=4] {'chan'}, dimensions={1} | all-to-all | bytes 131072 | tf_op jit(solution)/shard_map/all_to_all | solution.py:278
  9.7 0.7 copy.29
  10.4 5.8 %all-to-all-start.2 = ((bf16[8,32,128]{2,1,0:T(8,128)(2,1)}), bf16[8,32,128]{2,1,0:T(8,128)(2,1)S(1)}, u32[]{:S(2)}, u32[]{:S(2)}) async-start(bf16[8,32,128]{2,1,0:T(8,128)(2,1)} %bitcast.5), calls=%async_computation.2 | async-start | bytes 131072 | tf_op jit(solution)/shard_map/all_to_all | solution.py:280
  16.2 3.0 %pack.1 = bf16[256,3072]{1,0:T(8,128)(2,1)} custom-call(bf16[512,256]{1,0:T(8,128)(2,1)} %q_ref.1, bf16[512,256]{1,0:T(8,128)(2,1)} %k_ref.1, bf16[512,256]{1,0:T(8,128)(2,1)} %v_ref.1, bf16[512,256]{1,0:T(8,128)(2,1)} %g_ref.1, f32[512,256]{1,0:T(8,128)} %l_ref.1), custom_call_target="tpu_custom_call" | custom-call | tf_op jit(solution)/shard_map/pack/pallas_call | solution.py:270
  19.2 3.9 %all-to-all-done.2 = bf16[8,32,128]{2,1,0:T(8,128)(2,1)S(1)} async-done(((bf16[8,32,128]{2,1,0:T(8,128)(2,1)}), bf16[8,32,128]{2,1,0:T(8,128)(2,1)S(1)}, u32[]{:S(2)}, u32[]{:S(2)}) %all-to-all-start.2) | async-done | bytes 65568 | tf_op jit(solution)/shard_map/all_to_all | solution.py:280
  23.2 3.7 %all-to-all-start = ((bf16[8,32,3072]{2,1,0:T(8,128)(2,1)}), bf16[8,32,3072]{2,1,0:T(8,128)(2,1)S(1)}, u32[]{:S(2)}, u32[]{:S(2)}) async-start(bf16[8,32,3072]{2,1,0:T(8,128)(2,1)} %bitcast.28), calls=%async_computation | async-start | bytes 3145728 | tf_op jit(solution)/shard_map/all_to_all | solution.py:283
  26.9 0.0 copy-done
  26.9 0.1 constant_dynamic-slice_fusion
  27.0 0.1 copy.32
  27.1 0.8 copy.33
  27.8 0.0 copy-done.2
  27.8 0.1 constant_dynamic-slice_fusion.1
  27.9 0.1 tile.17
  28.0 0.6 copy.41
  28.6 0.0 copy-done.3
  28.6 1.0 copy.34.pos_ref
  29.7 0.6 copy_bitcast_fusion.s_ref
  30.3 32.3 %all-to-all-done = bf16[8,32,3072]{2,1,0:T(8,128)(2,1)S(1)} async-done(((bf16[8,32,3072]{2,1,0:T(8,128)(2,1)}), bf16[8,32,3072]{2,1,0:T(8,128)(2,1)S(1)}, u32[]{:S(2)}, u32[]{:S(2)}) %all-to-all-start) | async-done | bytes 1572896 | tf_op jit(solution)/shard_map/all_to_all | solution.py:283
  62.6 1.2 copy-done.1
  63.8 34.5 %operator.1 = bf16[256,3072]{1,0:T(8,128)(2,1)} custom-call(bf16[256,3072]{1,0:T(8,128)(2,1)} %bitcast.30, bf16[32,1024]{1,0:T(8,128)(2,1)} %copy_bitcast_fusion.s_ref, s32[1024,1]{1,0:T(8,128)} %copy.34.pos_ref, f32[2,24,128]{2,1,0:T(8,128)} %bitcast.36, f32[2,128,128]{2,1,0:T(8,128)} %bitcast.32, bf16[512,1024]{1,0:T(8,128)(2,1)} %constant.19.fh_ref, ...), custom_call_target="tpu_custom_call" | custom-call | tf_op jit(solution)/shard_map/operator/pallas_call | solution.py:309
  98.3 40.7 %all_to_all.35 = bf16[8,32,3072]{2,1,0:T(8,128)(2,1)} all-to-all(bf16[8,32,3072]{2,1,0:T(8,128)(2,1)} %bitcast.31), channel_id=1, replica_groups=mesh['seq'=8,'chan'=4] {'seq'}, dimensions={0} | all-to-all | bytes 3145728 | tf_op jit(solution)/shard_map/all_to_all | solution.py:318
  139.0 2.7 %unpack.1 = (bf16[512,256]{1,0:T(8,128)(2,1)}, bf16[512,256]{1,0:T(8,128)(2,1)}, bf16[512,256]{1,0:T(8,128)(2,1)}, bf16[512,256]{1,0:T(8,128)(2,1)}, f32[512,256]{1,0:T(8,128)}) custom-call(bf16[256,3072]{1,0:T(8,128)(2,1)} %bitcast.29), custom_call_target="tpu_custom_call" | custom-call | tf_op jit(solution)/shard_map/unpack/pallas_call | solution.py:321
  (6 shorter events, 0.0 us)
Async XLA Ops:
  0.6 26.2 %copy-start = (f32[128,256]{1,0:T(8,128)S(1)}, f32[128,256]{1,0:T(8,128)}, u32[]{:S(2)}) copy-start(f32[128,256]{1,0:T(8,128)} %param.14) | copy-start | bytes 393220
  10.4 12.7 %all-to-all-start.2 = ((bf16[8,32,128]{2,1,0:T(8,128)(2,1)}), bf16[8,32,128]{2,1,0:T(8,128)(2,1)S(1)}, u32[]{:S(2)}, u32[]{:S(2)}) async-start(bf16[8,32,128]{2,1,0:T(8,128)(2,1)} %bitcast.5), calls=%async_computation.2 | async-start | bytes 131072 | tf_op jit(solution)/shard_map/all_to_all | solution.py:280
  23.1 4.7 %copy-start.2 = (f32[3,7,256]{2,1,0:T(8,128)S(1)}, f32[3,7,256]{2,1,0:T(8,128)}, u32[]{:S(2)}) copy-start(f32[3,7,256]{2,1,0:T(8,128)} %param.13) | copy-start | bytes 64516
  23.1 5.5 %copy-start.3 = (s32[1024]{0:T(1024)S(1)}, s32[1024]{0:T(1024)}, u32[]{:S(2)}) copy-start(s32[1024]{0:T(1024)} %param.18) | copy-start | bytes 12292
  23.2 39.5 %all-to-all-start = ((bf16[8,32,3072]{2,1,0:T(8,128)(2,1)}), bf16[8,32,3072]{2,1,0:T(8,128)(2,1)S(1)}, u32[]{:S(2)}, u32[]{:S(2)}) async-start(bf16[8,32,3072]{2,1,0:T(8,128)(2,1)} %bitcast.28), calls=%async_computation | async-start | bytes 3145728 | tf_op jit(solution)/shard_map/all_to_all | solution.py:283
  62.6 1.2 copy-start.1

commit v2 on v1

v2 whole, which is shorter than its diff:
```python
import functools
import math

import jax
import jax.numpy as jnp
import numpy as np
from jax import lax
from jax.experimental import pallas as pl
from jax.experimental.pallas import tpu as pltpu
from jax.sharding import PartitionSpec as P

SHORT = 7
MED = 128
LANES = 128
f32 = jnp.float32
bf16 = jnp.bfloat16


def fourier(rows):
    full = 2 * rows
    order = np.concatenate([np.arange(0, rows, 2), np.arange(1, rows, 2)])
    time = np.arange(rows)
    angle = ((time[:, None] * order[None, :]) % full) * (2.0 * math.pi / full)
    real, imag = np.cos(angle), -np.sin(angle)
    imag[:, 0] = 1.0 - 2.0 * (time % 2)
    table = jnp.asarray(np.concatenate([real, imag], 1), f32)
    return table


def halves(x):
    high = x.astype(bf16)
    return high, (x - high.astype(f32)).astype(bf16)


def product(left, right, dims):
    (lh, ll), (rh, rl) = left, right
    dot = functools.partial(
        lax.dot_general, dimension_numbers=(dims, ((), ())), preferred_element_type=f32
    )
    return dot(lh, rh) + (dot(lh, rl) + dot(ll, rh))


def pack_kernel(q_ref, k_ref, v_ref, g_ref, s_ref, out_ref, landed, send_sem, recv_sem, own_sem):
    rows, lanes = q_ref.shape
    members = landed.shape[0]
    me = lax.axis_index("chan")

    def columns(who):
        return s_ref.at[:, pl.ds(pl.multiple_of(who * lanes, lanes), lanes)]

    own = pltpu.make_async_copy(columns(me), landed.at[me], own_sem)
    own.start()
    copies = []
    if members > 1:
        barrier = pltpu.get_barrier_semaphore()
        for step in range(1, members):
            peer = lax.rem(me + step, members)
            pl.semaphore_signal(
                barrier, inc=1, device_id={"chan": peer}, device_id_type=pl.DeviceIdType.MESH
            )
        pl.semaphore_wait(barrier, members - 1)
        for step in range(1, members):
            peer = lax.rem(me + step, members)
            copy = pltpu.make_async_remote_copy(
                src_ref=columns(peer),
                dst_ref=landed.at[me],
                send_sem=send_sem.at[step],
                recv_sem=recv_sem.at[step],
                device_id={"chan": peer},
                device_id_type=pl.DeviceIdType.MESH,
            )
            copy.start()
            copies.append(copy)
    for slot, ref in enumerate((q_ref, k_ref, v_ref, g_ref)):
        out_ref[:, slot * rows : (slot + 1) * rows] = ref[...].astype(f32).T.astype(bf16)
    own.wait()
    for copy in copies:
        copy.wait()
    stretch = jnp.concatenate([landed[j].astype(f32) for j in range(members)], 0)
    out_ref[:, 4 * rows :] = stretch.T.astype(bf16)


def pack_long_kernel(l_ref, out_ref):
    rows = l_ref.shape[0]
    high, low = halves(l_ref[...].T)
    out_ref[:, :rows] = high
    out_ref[:, rows:] = low


def unpack_kernel(in_ref, a_ref, b_ref):
    rows = a_ref.shape[0]
    a_ref[...] = in_ref[:, :rows].astype(f32).T.astype(bf16)
    b_ref[...] = in_ref[:, rows:].astype(f32).T.astype(bf16)


def unpack_long_kernel(in_ref, gl_ref):
    rows = gl_ref.shape[0]
    gl_ref[...] = (in_ref[:, :rows].astype(f32) + in_ref[:, rows:].astype(f32)).T


def from_before(tail, width):
    lane = lax.broadcasted_iota(jnp.int32, tail.shape, 1)
    return jnp.where(lane >= width, pltpu.roll(tail, width, 1), 0.0)


def from_after(head, width):
    lanes = head.shape[1]
    lane = lax.broadcasted_iota(jnp.int32, head.shape, 1)
    return jnp.where(lane < lanes - width, pltpu.roll(head, lanes - width, 1), 0.0)


def put(ref, start, value):
    for h in range(value.shape[1] // LANES):
        ref[h, start : start + value.shape[0], :] = value[:, h * LANES : (h + 1) * LANES]


def get(ref, start, size):
    return jnp.concatenate([ref[h, start : start + size, :] for h in range(ref.shape[0])], 1)


def taps_sum(src, taps, which, h, r, back):
    acc = jnp.zeros((LANES, LANES), f32)
    for j in range(SHORT):
        tap = taps[h, which * 8 + j : which * 8 + j + 1, :]
        lead = j if back else 8 - j
        acc = acc + tap * src[h, r + lead : r + lead + LANES, :]
    return acc


def short_causal(value, which, ext, taps, width, out, start):
    rows = value.shape[0]
    put(ext, 8, value)
    put(ext, 0, from_before(value[rows - 8 :], width))
    for h in range(ext.shape[0]):
        for r in range(0, rows, LANES):
            out[h, start + r : start + r + LANES, :] = taps_sum(ext, taps, which, h, r, False)


def short_anti(value, which, ext, taps, width, out, slot):
    rows = value.shape[0]
    put(ext, 0, value)
    put(ext, rows, from_after(value[:8], width))
    for h in range(ext.shape[0]):
        for r in range(0, rows, LANES):
            out[h * LANES : (h + 1) * LANES, slot * rows + r : slot * rows + r + LANES] = (
                taps_sum(ext, taps, which, h, r, True).T.astype(bf16)
            )


def medium(wide, turned, taps, out, back):
    tiles, size, _ = turned.shape[1:]
    steps = (size - MED) // LANES
    for s in range(8):
        for h in range(tiles):
            start = s if back else 8 - s
            turned[s, h, :, :] = wide[h, start : start + size, :]

    def step(n, carry):
        h = n // steps
        base = pl.multiple_of((n % steps) * LANES, LANES)
        acc = jnp.zeros((LANES, LANES), f32)
        for s in range(8):
            window = turned[s, h, pl.ds(base, LANES + MED), :]
            for m in range(MED // 8):
                lead = 8 * m if back else MED - 8 * m
                tap = taps[h, 8 * m + s : 8 * m + s + 1, :]
                acc = acc + tap * window[lead : lead + LANES]
        out[h, pl.ds(base, LANES), :] = acc
        return carry

    lax.fori_loop(0, tiles * steps, step, 0)


def keep(ref, signal, table, masked):
    count, _, width, rows = ref.shape
    spectrum = product(signal, table, ((1,), (0,)))
    real = spectrum[:, :rows].reshape(count, width, rows)
    imag = spectrum[:, rows:].reshape(count, width, rows)
    ref[:, 0] = real
    if not masked:
        ref[:, 1] = imag
        return
    first = lax.broadcasted_iota(jnp.int32, (count, width, rows), 2) == 0
    ref[:, 1] = jnp.where(first, 0.0, imag)
    ref[:, 2] = jnp.where(first, imag, real)


def emitter(us, width, rows, factor):
    lane = lax.broadcasted_iota(jnp.int32, (width, rows), 1)
    weight = jnp.where(lane == 0, 1.0, 2.0) * (factor / (2 * rows))
    sign = jnp.where(lane < rows // 2, 1.0, -1.0) * weight

    def emit(i, now, before):
        base = pl.multiple_of(i * width, width)
        us[pl.ds(base, width), 0:rows] = now[0] * weight + before[0] * sign
        us[pl.ds(base, width), rows : 2 * rows] = now[1] * weight + before[1] * sign

    return emit


def convolve(xs, ls, us):
    count, _, width, rows = xs.shape
    emit = emitter(us, width, rows, 1.0)
    zero = jnp.zeros((width, rows), f32)
    lane = lax.broadcasted_iota(jnp.int32, (width, rows), 1)

    def outer(i, before):
        def inner(b, total):
            xr, lr, li, lq = xs[i - b, 0], ls[b, 0], ls[b, 1], ls[b, 2]
            xi = jnp.where(lane == 0, xs[i - b, 2], xs[i - b, 1])
            return (total[0] + (xr * lr - xi * li), total[1] + (xr * li + xi * lq))

        now = lax.fori_loop(0, i + 1, inner, (zero, zero))
        emit(i, now, before)
        return now

    lax.fori_loop(0, count, outer, (zero, zero))


def correlate(ref, cs, us, factor):
    count, _, width, rows = ref.shape
    emit = emitter(us, width, rows, factor)
    zero = jnp.zeros((width, rows), f32)

    def outer(n, before):
        d = count - 1 - n

        def inner(b, total):
            cr, ci = cs[b + d, 0], cs[b + d, 1]
            ar, ai, aq = ref[b, 0], ref[b, 1], ref[b, 2]
            return (total[0] + (cr * ar + ci * ai), total[1] + (ci * aq - cr * ai))

        now = lax.fori_loop(0, n + 1, inner, (zero, zero))
        emit(d, now, before)
        return now

    lax.fori_loop(0, count, outer, (zero, zero))


def gates_kernel(
    scale, in_ref, pos_ref, st_ref, mt_ref, fh_ref, fl_ref,
    gl_ref, qs, ks, mid, og, xs, cs,
    ext, wide, turned, us,
):
    tiles = ext.shape[0]
    count, _, width, rows = xs.shape
    table = (fh_ref[...], fl_ref[...])

    def block(slot):
        return in_ref[:, slot * rows : (slot + 1) * rows].astype(f32).T

    short_causal(block(0), 0, ext, st_ref, width, qs, 0)
    short_causal(block(1), 1, ext, st_ref, width, ks, 0)
    short_causal(block(2), 2, ext, st_ref, width, wide, MED + 8)
    put(wide, 8, from_before(get(wide, 8 + rows, MED), width))
    for h in range(tiles):
        wide[h, 0:8, :] = jnp.zeros((8, LANES), f32)
    medium(wide, turned, mt_ref, mid, False)

    stretches = pos_ref.shape[0]
    stretch = jnp.concatenate(
        [in_ref[b * width : (b + 1) * width, 4 * rows :] for b in range(count)], 1
    )
    for a in range(count):
        spot = lax.broadcasted_iota(jnp.int32, (stretches, rows), 1) + a * rows
        onehot = (pos_ref[...] == spot).astype(f32).astype(bf16)
        placed = jnp.dot(stretch, onehot, preferred_element_type=f32)
        piece = in_ref[a * width : (a + 1) * width, 3 * rows : 4 * rows].astype(f32) + placed
        us[a * width : (a + 1) * width, 0:rows] = piece
    put(og, 0, us[:, 0:rows].T)

    keep(xs, halves((get(ks, 0, rows) * get(mid, 0, rows)).T), table, True)
    keep(cs, halves((get(og, 0, rows) * get(qs, 0, rows)).T), table, False)
    correlate(xs, cs, us, scale)
    high, low = halves(product(halves(us[...]), table, ((1,), (1,))))
    gl_ref[:, :rows] = high
    gl_ref[:, rows:] = low


def output_kernel(l_ref, xs, qs, og, st_ref, fh_ref, fl_ref, out_ref, ls, ext, us):
    _, _, width, rows = xs.shape
    table = (fh_ref[...], fl_ref[...])
    keep(ls, (l_ref[:, :rows], l_ref[:, rows:]), table, True)
    convolve(xs, ls, us)
    long_out = product(table, halves(us[...]), ((1,), (1,)))
    out_ref[:, 0:rows] = (get(qs, 0, rows) * long_out).T.astype(bf16)
    short_anti(get(og, 0, rows) * long_out, 0, ext, st_ref, width, out_ref, 1)


def back_kernel(ls, cs, ks, mid, st_ref, mt_ref, fh_ref, fl_ref, out_ref, ext, wide, turned, us, vb):
    _, _, width, rows = ls.shape
    table = (fh_ref[...], fl_ref[...])
    correlate(ls, cs, us, 1.0)
    inner_grad = product(table, halves(us[...]), ((1,), (1,)))
    mid_back = inner_grad * get(ks, 0, rows)
    put(wide, 0, mid_back)
    put(wide, rows, from_after(mid_back[:MED], width))
    for h in range(ext.shape[0]):
        wide[h, rows + MED : rows + MED + 8, :] = jnp.zeros((8, LANES), f32)
    short_anti(inner_grad * get(mid, 0, rows), 1, ext, st_ref, width, out_ref, 0)
    medium(wide, turned, mt_ref, vb, True)
    short_anti(get(vb, 0, rows), 2, ext, st_ref, width, out_ref, 1)


def whole_spec(n):
    return [pl.BlockSpec(memory_space=pltpu.VMEM)] * n


def local(
    q_proj, k_proj, v_proj, short_taps, medium_taps, long_taps, grad_out, stretch_grads, positions
):
    rows, lanes = q_proj.shape
    count = lax.axis_size("seq")
    index = lax.axis_index("seq")
    width = lanes // count
    tiles = lanes // LANES

    shape = jax.ShapeDtypeStruct

    def call(kernel, outs, args, scratch=(), micros=3):
        many = len(outs) > 1
        return pl.pallas_call(
            kernel,
            out_shape=outs if many else outs[0],
            in_specs=whole_spec(len(args)),
            out_specs=whole_spec(len(outs)) if many else whole_spec(1)[0],
            scratch_shapes=list(scratch),
            cost_estimate=pl.CostEstimate(
                flops=micros * 10**9, bytes_accessed=micros * 3 * 10**6, transcendentals=0
            ),
        )(*args)

    def regroup(array):
        split = array.reshape(count, width, array.shape[1])
        moved = lax.all_to_all(split, "seq", split_axis=0, concat_axis=0, tiled=True)
        return moved.reshape(array.shape)

    pair = shape((lanes, 2 * rows), bf16)
    signal = shape((tiles, rows, LANES), f32)
    three = shape((count, 3, width, rows), f32)
    two = shape((count, 2, width, rows), f32)
    ext = pltpu.VMEM((tiles, rows + 8, LANES), f32)
    wide = pltpu.VMEM((tiles, rows + MED + 8, LANES), f32)
    turned = pltpu.VMEM((8, tiles, rows + MED, LANES), f32)
    spectrum = pltpu.VMEM((lanes, 2 * rows), f32)

    members = lax.axis_size("chan")
    stretches = stretch_grads.shape[0]
    packed = pl.pallas_call(
        pack_kernel,
        out_shape=shape((lanes, 4 * rows + members * stretches), bf16),
        in_specs=whole_spec(5),
        out_specs=whole_spec(1)[0],
        scratch_shapes=[
            pltpu.VMEM((members, stretches, lanes), bf16),
            pltpu.SemaphoreType.DMA((members,)),
            pltpu.SemaphoreType.DMA((members,)),
            pltpu.SemaphoreType.DMA,
        ],
        compiler_params=pltpu.CompilerParams(
            collective_id=0 if members > 1 else None, has_side_effects=True
        ),
        name="pack",
    )(q_proj, k_proj, v_proj, grad_out, stretch_grads)
    arrived = regroup(packed)
    long_packed = call(pack_long_kernel, [pair], (long_taps,))
    long_arrived = regroup(long_packed)

    def spread(taps):
        part = lax.dynamic_slice_in_dim(taps, index * width, width, 1)
        part = jnp.tile(part, (1, count))
        return part.reshape(taps.shape[0], tiles, LANES).transpose(1, 0, 2)

    short = spread(jnp.pad(short_taps, ((0, 0), (0, 1), (0, 0))).reshape(24, lanes))
    medium_part = spread(medium_taps)
    fh, fl = halves(fourier(rows))
    gl, qs, ks, mid, og, xs, cs = call(
        functools.partial(gates_kernel, (rows * count) ** (-0.5)),
        [pair, signal, signal, signal, signal, three, two],
        (arrived, positions[:, None], short, medium_part, fh, fl),
        (ext, wide, turned, spectrum),
        20,
    )
    gl_back = regroup(gl)
    y_gq, ls = call(
        output_kernel, [pair, three], (long_arrived, xs, qs, og, short, fh, fl), (ext, spectrum), 8
    )
    y_back = regroup(y_gq)
    gk_gv = call(
        back_kernel,
        [pair],
        (ls, cs, ks, mid, short, medium_part, fh, fl),
        (ext, wide, turned, spectrum, pltpu.VMEM((tiles, rows, LANES), f32)),
        12,
    )
    k_back = regroup(gk_gv)
    half = shape((rows, lanes), bf16)
    grad_long = call(unpack_long_kernel, [shape((rows, lanes), f32)], (gl_back,))
    y_out, grad_q = call(unpack_kernel, [half, half], (y_back,))
    grad_k, grad_v = call(unpack_kernel, [half, half], (k_back,))
    return (y_out, grad_q, grad_k, grad_v, grad_long)


def solution(mesh):
    return jax.shard_map(
        local,
        mesh=mesh,
        in_specs=(
            P("seq", "chan"),
            P("seq", "chan"),
            P("seq", "chan"),
            P(None, None, "chan"),
            P(None, "chan"),
            P("seq", "chan"),
            P("seq", "chan"),
            P(("seq", "chan"), None),
            P(),
        ),
        out_specs=(
            P("seq", "chan"),
            P("seq", "chan"),
            P("seq", "chan"),
            P("seq", "chan"),
            P("seq", "chan"),
        ),
        check_vma=False,
    )
```

time: 142 us -> 146 us (1.028)
  Pallas kernels: 40.2 us -> 55.8 us
  blocking collectives: 48.9 us -> 37.8 us
  starting transfers between devices: 9.52 us -> 13.4 us
  waiting for transfers between devices: 36.3 us -> 32.8 us
  local copies, waits for them, and re-layouts: 6.16 us -> 4.35 us
    pallas_call x3 -> x8, Pallas kernels: 40.2 us -> 55.8 us  [the longest x7 48.5 us: call(): pl.pallas_call(kernel, out_shape=outs if many else outs[0], in_specs=whol...]
    all_to_all x2, blocking collectives: 48.9 us -> 37.8 us  [regroup(): lax.all_to_all(split, 'seq', split_axis=0, concat_axis=0, tiled=True)]
    all_to_all x2 -> x3, starting transfers between devices: 9.52 us -> 13.4 us  [regroup(): lax.all_to_all(split, 'seq', split_axis=0, concat_axis=0, tiled=True)]
    all_to_all x2 -> x3, waiting for transfers between devices: 36.3 us -> 32.8 us  [regroup(): lax.all_to_all(split, 'seq', split_axis=0, concat_axis=0, tiled=True)]
  transfers between devices with their start and end apart: 2 -> 3, of which waited for: 2 -> 2; matrix products, arithmetic and copies ran while one was open for 2% -> 2% of each run, Pallas kernels for 2% -> 17%
where the time goes in v2:
time: 146 us; the launch traced here: 145 us
  Pallas kernels  55.8 us (38%)
  blocking collectives  37.8 us (26%)
  waiting for transfers between devices  32.8 us (22%)
  starting transfers between devices  13.4 us (9%)
  local copies, waits for them, and re-layouts  4.35 us (3%)
    pallas_call x7, Pallas kernels, call(): pl.pallas_call(kernel, out_shape=outs if many else outs[0], in_specs=whol...  48.5 us
    all_to_all x2, blocking collectives, regroup(): lax.all_to_all(split, 'seq', split_axis=0, concat_axis=0, tiled=True)  37.8 us
    all_to_all x3, waiting for transfers between devices, regroup(): lax.all_to_all(split, 'seq', split_axis=0, concat_axis=0, tiled=True)  32.8 us
    all_to_all x3, starting transfers between devices, regroup(): lax.all_to_all(split, 'seq', split_axis=0, concat_axis=0, tiled=True)  13.4 us
    pallas_call x1, Pallas kernels, local(): pl.pallas_call(pack_kernel, out_shape=shape((lanes, 4 * rows + members *...  7.32 us
  transfers between devices with their start and end apart: 3, of which 2 were waited for; matrix products, arithmetic and copies ran while one was open for 2% of the time, Pallas kernels for 17%

profile of v2, /device:TPU:0, one launch (start us, length us, event | category | flops | bytes accessed | tf_op | source)
XLA Modules:
  0.0 144.9 jit_solution(12380968709075191380)
XLA Ops:
  0.6 7.3 %pack.1 = bf16[256,2176]{1,0:T(8,128)(2,1)} custom-call(bf16[512,256]{1,0:T(8,128)(2,1)} %q_ref.1, bf16[512,256]{1,0:T(8,128)(2,1)} %k_ref.1, bf16[512,256]{1,0:T(8,128)(2,1)} %v_ref.1, bf16[512,256]{1,0:T(8,128)(2,1)} %g_ref.1, bf16[32,1024]{1,0:T(8,128)(2,1)} %s_ref.1), custom_call_target="tpu_custom_call" | custom-call | tf_op jit(solution)/shard_map/pack/pallas_call | solution.py:349
  8.0 6.2 %all-to-all-start.1 = ((bf16[8,32,2176]{2,1,0:T(8,128)(2,1)}), bf16[8,32,2176]{2,1,0:T(8,128)(2,1)S(1)}, u32[]{:S(2)}, u32[]{:S(2)}) async-start(bf16[8,32,2176]{2,1,0:T(8,128)(2,1)} %bitcast.18), calls=%async_computation.1 | async-start | bytes 2228224 | tf_op jit(solution)/shard_map/all_to_all | solution.py:335
  14.2 0.1 constant_dynamic-slice_fusion
  14.2 0.1 copy.16
  14.3 0.1 constant_dynamic-slice_fusion.1
  14.4 0.1 tile.17
  14.5 0.6 copy.20
  15.2 0.8 copy.17
  15.9 1.0 copy.18.pos_ref
  16.9 2.0 %shard_map.137 = bf16[256,1024]{1,0:T(8,128)(2,1)} custom-call(f32[512,256]{1,0:T(8,128)} %l_ref.1), custom_call_target="tpu_custom_call" | custom-call | flops 3000000000 | bytes 9000000 | tf_op jit(solution)/shard_map/pallas_call | solution.py:322
  19.0 22.6 %all-to-all-done.1 = bf16[8,32,2176]{2,1,0:T(8,128)(2,1)S(1)} async-done(((bf16[8,32,2176]{2,1,0:T(8,128)(2,1)}), bf16[8,32,2176]{2,1,0:T(8,128)(2,1)S(1)}, u32[]{:S(2)}, u32[]{:S(2)}) %all-to-all-start.1) | async-done | bytes 1114144 | tf_op jit(solution)/shard_map/all_to_all | solution.py:335
  41.6 3.6 %all-to-all-start = ((bf16[8,32,1024]{2,1,0:T(8,128)(2,1)}), bf16[8,32,1024]{2,1,0:T(8,128)(2,1)S(1)}, u32[]{:S(2)}, u32[]{:S(2)}) async-start(bf16[8,32,1024]{2,1,0:T(8,128)(2,1)} %bitcast.21), calls=%async_computation | async-start | bytes 1048576 | tf_op jit(solution)/shard_map/all_to_all | solution.py:335
  45.2 18.4 %shard_map.138 = (bf16[256,1024]{1,0:T(8,128)(2,1)}, f32[2,512,128]{2,1,0:T(8,128)}, f32[2,512,128]{2,1,0:T(8,128)}, f32[2,512,128]{2,1,0:T(8,128)}, f32[2,512,1...) custom-call(bf16[256,2176]{1,0:T(8,128)(2,1)} %bitcast.19, s32[1024,1]{1,0:T(8,128)} %copy.18.pos_ref, ...), custom_call_target="tpu_custom_call" | custom-call | flops 20000000000 | bytes 60000000 | tf_op jit(solution)/shard_map/pallas_call | solution.py:322
  63.7 0.8 copy-done.2
  64.5 7.1 %shard_map.139 = (bf16[256,1024]{1,0:T(8,128)(2,1)}, f32[8,3,32,512]{3,2,1,0:T(8,128)}) custom-call(bf16[256,1024]{1,0:T(8,128)(2,1)} %bitcast.20, f32[8,3,32,512]{3,2,1,0:T(8,128)} %get-tuple-element.18.xs, f32[2,512,128]{2,1,0:T(8,128)} %get-tuple-element.19.qs, f32[2,512,128]{2,1,0:T(8,128)} %get-tuple-element.20.og, f32[2,24,128]{2,1,0:T(8,128)} %bitcast.31, ...), custom_call_target="tpu_custom_call" | custom-call | flops 8000000000 | bytes 24000000 | tf_op jit(solution)/shard_map/pallas_call | solution.py:322
  71.6 14.9 %shard_map.141 = bf16[256,1024]{1,0:T(8,128)(2,1)} custom-call(f32[8,3,32,512]{3,2,1,0:T(8,128)} %get-tuple-element.24.ls, f32[8,2,32,512]{3,2,1,0:T(8,128)} %get-tuple-element.25.cs, f32[2,512,128]{2,1,0:T(8,128)} %get-tuple-element.26.ks, f32[2,512,128]{2,1,0:T(8,128)} %get-tuple-element.27.mid, f32[2,24,128]{2,1,0:T(8,128)} %bitcast.32, ...), custom_call_target="tpu_custom_call" | custom-call | flops 12000000000 | bytes 36000000 | tf_op jit(solution)/shard_map/pallas_call | solution.py:322
  86.5 20.2 %all_to_all.25 = bf16[8,32,1024]{2,1,0:T(8,128)(2,1)} all-to-all(bf16[8,32,1024]{2,1,0:T(8,128)(2,1)} %bitcast.26), channel_id=1, replica_groups=mesh['seq'=8,'chan'=4] {'seq'}, dimensions={0} | all-to-all | bytes 1048576 | tf_op jit(solution)/shard_map/all_to_all | solution.py:335
  106.7 17.6 %all_to_all.26 = bf16[8,32,1024]{2,1,0:T(8,128)(2,1)} all-to-all(bf16[8,32,1024]{2,1,0:T(8,128)(2,1)S(1)} %bitcast.23), channel_id=1, replica_groups=mesh['seq'=8,'chan'=4] {'seq'}, dimensions={0} | all-to-all | bytes 1048576 | tf_op jit(solution)/shard_map/all_to_all | solution.py:335
  124.3 3.6 %all-to-all-start.4 = ((bf16[8,32,1024]{2,1,0:T(8,128)(2,1)}), bf16[8,32,1024]{2,1,0:T(8,128)(2,1)S(1)}, u32[]{:S(2)}, u32[]{:S(2)}) async-start(bf16[8,32,1024]{2,1,0:T(8,128)(2,1)} %bitcast.13), calls=%async_computation.4 | async-start | bytes 1048576 | tf_op jit(solution)/shard_map/all_to_all | solution.py:335
  127.9 2.0 %shard_map.142 = (bf16[512,256]{1,0:T(8,128)(2,1)}, bf16[512,256]{1,0:T(8,128)(2,1)}) custom-call(bf16[256,1024]{1,0:T(8,128)(2,1)} %bitcast.25), custom_call_target="tpu_custom_call" | custom-call | flops 3000000000 | bytes 9000000 | tf_op jit(solution)/shard_map/pallas_call | solution.py:322
  129.9 2.0 %shard_map.140 = (bf16[512,256]{1,0:T(8,128)(2,1)}, bf16[512,256]{1,0:T(8,128)(2,1)}) custom-call(bf16[256,1024]{1,0:T(8,128)(2,1)} %bitcast.24), custom_call_target="tpu_custom_call" | custom-call | flops 3000000000 | bytes 9000000 | tf_op jit(solution)/shard_map/pallas_call | solution.py:322
  131.9 10.2 %all-to-all-done.4 = bf16[8,32,1024]{2,1,0:T(8,128)(2,1)S(1)} async-done(((bf16[8,32,1024]{2,1,0:T(8,128)(2,1)}), bf16[8,32,1024]{2,1,0:T(8,128)(2,1)S(1)}, u32[]{:S(2)}, u32[]{:S(2)}) %all-to-all-start.4) | async-done | bytes 524320 | tf_op jit(solution)/shard_map/all_to_all | solution.py:335
  142.0 0.8 copy-done.3
  142.8 2.0 %shard_map.143 = f32[512,256]{1,0:T(8,128)} custom-call(bf16[256,1024]{1,0:T(8,128)(2,1)} %bitcast.22), custom_call_target="tpu_custom_call" | custom-call | flops 3000000000 | bytes 9000000 | tf_op jit(solution)/shard_map/pallas_call | solution.py:322
  (16 shorter events, 0.1 us)
Async XLA Ops:
  0.6 13.5 %copy-start = (f32[128,256]{1,0:T(8,128)S(1)}, f32[128,256]{1,0:T(8,128)}, u32[]{:S(2)}) copy-start(f32[128,256]{1,0:T(8,128)} %param.14) | copy-start | bytes 393220
  8.0 6.3 %copy-start.5 = (f32[3,7,256]{2,1,0:T(8,128)S(1)}, f32[3,7,256]{2,1,0:T(8,128)}, u32[]{:S(2)}) copy-start(f32[3,7,256]{2,1,0:T(8,128)} %param.13) | copy-start | bytes 64516
  8.0 7.9 %copy-start.6 = (s32[1024]{0:T(1024)S(1)}, s32[1024]{0:T(1024)}, u32[]{:S(2)}) copy-start(s32[1024]{0:T(1024)} %param.18) | copy-start | bytes 12292
  8.0 33.6 %all-to-all-start.1 = ((bf16[8,32,2176]{2,1,0:T(8,128)(2,1)}), bf16[8,32,2176]{2,1,0:T(8,128)(2,1)S(1)}, u32[]{:S(2)}, u32[]{:S(2)}) async-start(bf16[8,32,2176]{2,1,0:T(8,128)(2,1)} %bitcast.18), calls=%async_computation.1 | async-start | bytes 2228224 | tf_op jit(solution)/shard_map/all_to_all | solution.py:335
  41.6 3.6 %copy-start.1 = (bf16[8,32,2176]{2,1,0:T(8,128)(2,1)}, bf16[8,32,2176]{2,1,0:T(8,128)(2,1)S(1)}, u32[]{:S(2)}) copy-start(bf16[8,32,2176]{2,1,0:T(8,128)(2,1)S(1)} %all-to-all-done.1) | copy-start | bytes 3342340
  41.6 22.0 %all-to-all-start = ((bf16[8,32,1024]{2,1,0:T(8,128)(2,1)}), bf16[8,32,1024]{2,1,0:T(8,128)(2,1)S(1)}, u32[]{:S(2)}, u32[]{:S(2)}) async-start(bf16[8,32,1024]{2,1,0:T(8,128)(2,1)} %bitcast.21), calls=%async_computation | async-start | bytes 1048576 | tf_op jit(solution)/shard_map/all_to_all | solution.py:335
  63.7 0.8 copy-start.2
  71.6 35.1 %copy-start.4 = (bf16[256,1024]{1,0:T(8,128)(2,1)S(1)}, bf16[256,1024]{1,0:T(8,128)(2,1)}, u32[]{:S(2)}) copy-start(bf16[256,1024]{1,0:T(8,128)(2,1)} %get-tuple-element.21) | copy-start | bytes 1572868
  124.3 17.7 %all-to-all-start.4 = ((bf16[8,32,1024]{2,1,0:T(8,128)(2,1)}), bf16[8,32,1024]{2,1,0:T(8,128)(2,1)S(1)}, u32[]{:S(2)}, u32[]{:S(2)}) async-start(bf16[8,32,1024]{2,1,0:T(8,128)(2,1)} %bitcast.13), calls=%async_computation.4 | async-start | bytes 1048576 | tf_op jit(solution)/shard_map/all_to_all | solution.py:335
  142.0 0.8 copy-start.3

commit v3 on v2

--- a/solution.py
+++ b/solution.py
@@ -40,7 +40,7 @@
     return dot(lh, rh) + (dot(lh, rl) + dot(ll, rh))
 
 
-def pack_kernel(q_ref, k_ref, v_ref, g_ref, s_ref, out_ref, landed, send_sem, recv_sem, own_sem):
+def pack_kernel(q_ref, g_ref, l_ref, s_ref, out_ref, landed, send_sem, recv_sem, own_sem):
     rows, lanes = q_ref.shape
     members = landed.shape[0]
     me = lax.axis_index("chan")
@@ -71,8 +71,11 @@
             )
             copy.start()
             copies.append(copy)
-    for slot, ref in enumerate((q_ref, k_ref, v_ref, g_ref)):
+    for slot, ref in enumerate((q_ref, g_ref)):
         out_ref[:, slot * rows : (slot + 1) * rows] = ref[...].astype(f32).T.astype(bf16)
+    high, low = halves(l_ref[...].T)
+    out_ref[:, 2 * rows : 3 * rows] = high
+    out_ref[:, 3 * rows : 4 * rows] = low
     own.wait()
     for copy in copies:
         copy.wait()
@@ -80,11 +83,10 @@
     out_ref[:, 4 * rows :] = stretch.T.astype(bf16)
 
 
-def pack_long_kernel(l_ref, out_ref):
-    rows = l_ref.shape[0]
-    high, low = halves(l_ref[...].T)
-    out_ref[:, :rows] = high
-    out_ref[:, rows:] = low
+def pack_first_kernel(k_ref, v_ref, out_ref):
+    rows = k_ref.shape[0]
+    out_ref[:, :rows] = k_ref[...].astype(f32).T.astype(bf16)
+    out_ref[:, rows:] = v_ref[...].astype(f32).T.astype(bf16)
 
 
 def unpack_kernel(in_ref, a_ref, b_ref):
@@ -237,26 +239,23 @@
     lax.fori_loop(0, count, outer, (zero, zero))
 
 
-def gates_kernel(
-    scale, in_ref, pos_ref, st_ref, mt_ref, fh_ref, fl_ref,
-    gl_ref, qs, ks, mid, og, xs, cs,
-    ext, wide, turned, us,
-):
+def filters_kernel(in_ref, st_ref, mt_ref, fh_ref, fl_ref, ks, mid, xs, ext, wide, turned):
     tiles = ext.shape[0]
-    count, _, width, rows = xs.shape
+    _, _, width, rows = xs.shape
     table = (fh_ref[...], fl_ref[...])
-
-    def block(slot):
-        return in_ref[:, slot * rows : (slot + 1) * rows].astype(f32).T
-
-    short_causal(block(0), 0, ext, st_ref, width, qs, 0)
-    short_causal(block(1), 1, ext, st_ref, width, ks, 0)
-    short_causal(block(2), 2, ext, st_ref, width, wide, MED + 8)
+    short_causal(in_ref[:, :rows].astype(f32).T, 1, ext, st_ref, width, ks, 0)
+    short_causal(in_ref[:, rows:].astype(f32).T, 2, ext, st_ref, width, wide, MED + 8)
     put(wide, 8, from_before(get(wide, 8 + rows, MED), width))
     for h in range(tiles):
         wide[h, 0:8, :] = jnp.zeros((8, LANES), f32)
     medium(wide, turned, mt_ref, mid, False)
-
+    keep(xs, halves((get(ks, 0, rows) * get(mid, 0, rows)).T), table, True)
+
+
+def gates_kernel(scale, in_ref, pos_ref, st_ref, fh_ref, fl_ref, xs, gl_ref, qs, og, cs, ext, us):
+    count, _, width, rows = xs.shape
+    table = (fh_ref[...], fl_ref[...])
+    short_causal(in_ref[:, :rows].astype(f32).T, 0, ext, st_ref, width, qs, 0)
     stretches = pos_ref.shape[0]
     stretch = jnp.concatenate(
         [in_ref[b * width : (b + 1) * width, 4 * rows :] for b in range(count)], 1
@@ -265,11 +264,10 @@
         spot = lax.broadcasted_iota(jnp.int32, (stretches, rows), 1) + a * rows
         onehot = (pos_ref[...] == spot).astype(f32).astype(bf16)
         placed = jnp.dot(stretch, onehot, preferred_element_type=f32)
-        piece = in_ref[a * width : (a + 1) * width, 3 * rows : 4 * rows].astype(f32) + placed
+        piece = in_ref[a * width : (a + 1) * width, rows : 2 * rows].astype(f32) + placed
         us[a * width : (a + 1) * width, 0:rows] = piece
     put(og, 0, us[:, 0:rows].T)
 
-    keep(xs, halves((get(ks, 0, rows) * get(mid, 0, rows)).T), table, True)
     keep(cs, halves((get(og, 0, rows) * get(qs, 0, rows)).T), table, False)
     correlate(xs, cs, us, scale)
     high, low = halves(product(halves(us[...]), table, ((1,), (1,))))
@@ -280,7 +278,7 @@
 def output_kernel(l_ref, xs, qs, og, st_ref, fh_ref, fl_ref, out_ref, ls, ext, us):
     _, _, width, rows = xs.shape
     table = (fh_ref[...], fl_ref[...])
-    keep(ls, (l_ref[:, :rows], l_ref[:, rows:]), table, True)
+    keep(ls, (l_ref[:, 2 * rows : 3 * rows], l_ref[:, 3 * rows : 4 * rows]), table, True)
     convolve(xs, ls, us)
     long_out = product(table, halves(us[...]), ((1,), (1,)))
     out_ref[:, 0:rows] = (get(qs, 0, rows) * long_out).T.astype(bf16)
@@ -344,12 +342,14 @@
     turned = pltpu.VMEM((8, tiles, rows + MED, LANES), f32)
     spectrum = pltpu.VMEM((lanes, 2 * rows), f32)
 
+    first_packed = call(pack_first_kernel, [pair], (k_proj, v_proj))
+    first_arrived = regroup(first_packed)
     members = lax.axis_size("chan")
     stretches = stretch_grads.shape[0]
     packed = pl.pallas_call(
         pack_kernel,
         out_shape=shape((lanes, 4 * rows + members * stretches), bf16),
-        in_specs=whole_spec(5),
+        in_specs=whole_spec(4),
         out_specs=whole_spec(1)[0],
         scratch_shapes=[
             pltpu.VMEM((members, stretches, lanes), bf16),
@@ -361,10 +361,8 @@
             collective_id=0 if members > 1 else None, has_side_effects=True
         ),
         name="pack",
-    )(q_proj, k_proj, v_proj, grad_out, stretch_grads)
+    )(q_proj, grad_out, long_taps, stretch_grads)
     arrived = regroup(packed)
-    long_packed = call(pack_long_kernel, [pair], (long_taps,))
-    long_arrived = regroup(long_packed)
 
     def spread(taps):
         part = lax.dynamic_slice_in_dim(taps, index * width, width, 1)
@@ -374,16 +372,23 @@
     short = spread(jnp.pad(short_taps, ((0, 0), (0, 1), (0, 0))).reshape(24, lanes))
     medium_part = spread(medium_taps)
     fh, fl = halves(fourier(rows))
-    gl, qs, ks, mid, og, xs, cs = call(
+    ks, mid, xs = call(
+        filters_kernel,
+        [signal, signal, three],
+        (first_arrived, short, medium_part, fh, fl),
+        (ext, wide, turned),
+        10,
+    )
+    gl, qs, og, cs = call(
         functools.partial(gates_kernel, (rows * count) ** (-0.5)),
-        [pair, signal, signal, signal, signal, three, two],
-        (arrived, positions[:, None], short, medium_part, fh, fl),
-        (ext, wide, turned, spectrum),
-        20,
+        [pair, signal, signal, two],
+        (arrived, positions[:, None], short, fh, fl, xs),
+        (ext, spectrum),
+        10,
     )
     gl_back = regroup(gl)
     y_gq, ls = call(
-        output_kernel, [pair, three], (long_arrived, xs, qs, og, short, fh, fl), (ext, spectrum), 8
+        output_kernel, [pair, three], (arrived, xs, qs, og, short, fh, fl), (ext, spectrum), 8
     )
     y_back = regroup(y_gq)
     gk_gv = call(

time: 146 us -> 145 us (level)
  waiting for transfers between devices: 32.8 us -> 30.3 us
  Pallas kernels: 55.8 us -> 58 us
  blocking collectives: 37.8 us -> 36.1 us
    pallas_call x7 -> x8, Pallas kernels: 48.5 us -> 51.9 us  [call(): pl.pallas_call(kernel, out_shape=outs if many else outs[0], in_specs=whol...]
    all_to_all x3, waiting for transfers between devices: 32.8 us -> 30.3 us  [regroup(): lax.all_to_all(split, 'seq', split_axis=0, concat_axis=0, tiled=True)]
    all_to_all x2, blocking collectives: 37.8 us -> 36.1 us  [regroup(): lax.all_to_all(split, 'seq', split_axis=0, concat_axis=0, tiled=True)]
  transfers between devices with their start and end apart: 3 -> 3, of which waited for: 2 -> 3; matrix products, arithmetic and copies ran while one was open for 2% -> 2% of each run, Pallas kernels for 17% -> 16%
where the time goes in v3:
time: 145 us; the launch traced here: 144 us
  Pallas kernels  58 us (40%)
  blocking collectives  36.1 us (25%)
  waiting for transfers between devices  30.3 us (21%)
  starting transfers between devices  14.7 us (10%)
  local copies, waits for them, and re-layouts  4.57 us (3%)
    pallas_call x8, Pallas kernels, call(): pl.pallas_call(kernel, out_shape=outs if many else outs[0], in_specs=whol...  51.9 us
    all_to_all x2, blocking collectives, regroup(): lax.all_to_all(split, 'seq', split_axis=0, concat_axis=0, tiled=True)  36.1 us
    all_to_all x3, waiting for transfers between devices, regroup(): lax.all_to_all(split, 'seq', split_axis=0, concat_axis=0, tiled=True)  30.3 us
    all_to_all x3, starting transfers between devices, regroup(): lax.all_to_all(split, 'seq', split_axis=0, concat_axis=0, tiled=True)  14.7 us
    pallas_call x1, Pallas kernels, local(): pl.pallas_call(pack_kernel, out_shape=shape((lanes, 4 * rows + members *...  6.13 us
  transfers between devices with their start and end apart: 3, of which 3 were waited for; matrix products, arithmetic and copies ran while one was open for 2% of the time, Pallas kernels for 16%

profile of v3, /device:TPU:0, one launch (start us, length us, event | category | flops | bytes accessed | tf_op | source)
XLA Modules:
  0.0 144.3 jit_solution(12322428734783157206)
XLA Ops:
  0.6 2.1 %shard_map.137 = bf16[256,1024]{1,0:T(8,128)(2,1)} custom-call(bf16[512,256]{1,0:T(8,128)(2,1)} %k_ref.1, bf16[512,256]{1,0:T(8,128)(2,1)} %v_ref.1), custom_call_target="tpu_custom_call" | custom-call | flops 3000000000 | bytes 9000000 | tf_op jit(solution)/shard_map/pallas_call | solution.py:320
  2.7 7.3 %all-to-all-start.1 = ((bf16[8,32,1024]{2,1,0:T(8,128)(2,1)}), bf16[8,32,1024]{2,1,0:T(8,128)(2,1)S(1)}, u32[]{:S(2)}, u32[]{:S(2)}) async-start(bf16[8,32,1024]{2,1,0:T(8,128)(2,1)} %bitcast.27), calls=%async_computation.1 | async-start | bytes 1048576 | tf_op jit(solution)/shard_map/all_to_all | solution.py:333
  10.0 6.1 %pack.1 = bf16[256,2176]{1,0:T(8,128)(2,1)} custom-call(bf16[512,256]{1,0:T(8,128)(2,1)} %q_ref.1, bf16[512,256]{1,0:T(8,128)(2,1)} %g_ref.1, f32[512,256]{1,0:T(8,128)} %l_ref.1, bf16[32,1024]{1,0:T(8,128)(2,1)} %s_ref.1), custom_call_target="tpu_custom_call" | custom-call | tf_op jit(solution)/shard_map/pack/pallas_call | solution.py:349
  16.1 8.3 %all-to-all-done.1 = bf16[8,32,1024]{2,1,0:T(8,128)(2,1)S(1)} async-done(((bf16[8,32,1024]{2,1,0:T(8,128)(2,1)}), bf16[8,32,1024]{2,1,0:T(8,128)(2,1)S(1)}, u32[]{:S(2)}, u32[]{:S(2)}) %all-to-all-start.1) | async-done | bytes 524320 | tf_op jit(solution)/shard_map/all_to_all | solution.py:333
  24.5 3.8 %all-to-all-start = ((bf16[8,32,2176]{2,1,0:T(8,128)(2,1)}), bf16[8,32,2176]{2,1,0:T(8,128)(2,1)S(1)}, u32[]{:S(2)}, u32[]{:S(2)}) async-start(bf16[8,32,2176]{2,1,0:T(8,128)(2,1)} %bitcast.18), calls=%async_computation | async-start | bytes 2228224 | tf_op jit(solution)/shard_map/all_to_all | solution.py:333
  28.3 0.1 constant_dynamic-slice_fusion
  28.5 0.1 tile.17
  28.6 0.6 copy.20
  29.2 0.8 copy.17
  30.0 1.0 copy.18.pos_ref
  31.0 12.8 %shard_map.138 = (f32[2,512,128]{2,1,0:T(8,128)}, f32[2,512,128]{2,1,0:T(8,128)}, f32[8,3,32,512]{3,2,1,0:T(8,128)}) custom-call(bf16[256,1024]{1,0:T(8,128)(2,1)} %bitcast.21, f32[2,24,128]{2,1,0:T(8,128)} %bitcast.31, f32[2,128,128]{2,1,0:T(8,128)} %bitcast.29, bf16[512,1024]{1,0:T(8,128)(2,1)} %constant.19.fh_ref, bf16[512,1024]{1,0:T(8,128)(2,1)} %constant.22.fl_ref), custom_call_target="tpu_custom_call" | custom-call | flops 10000000000 | bytes 30000000 | tf_op jit(solution)/shard_map/pallas_call | solution.py:320
  43.9 11.7 %all-to-all-done = bf16[8,32,2176]{2,1,0:T(8,128)(2,1)S(1)} async-done(((bf16[8,32,2176]{2,1,0:T(8,128)(2,1)}), bf16[8,32,2176]{2,1,0:T(8,128)(2,1)S(1)}, u32[]{:S(2)}, u32[]{:S(2)}) %all-to-all-start) | async-done | bytes 1114144 | tf_op jit(solution)/shard_map/all_to_all | solution.py:333
  55.6 1.0 copy-done.1
  56.6 8.9 %shard_map.139 = (bf16[256,1024]{1,0:T(8,128)(2,1)}, f32[2,512,128]{2,1,0:T(8,128)}, f32[2,512,128]{2,1,0:T(8,128)}, f32[8,2,32,512]{3,2,1,0:T(8,128)}) custom-call(bf16[256,2176]{1,0:T(8,128)(2,1)} %bitcast.19, s32[1024,1]{1,0:T(8,128)} %copy.18.pos_ref, f32[2,24,128]{2,1,0:T(8,128)} %bitcast.32, bf16[512,1024]{1,0:T(8,128)(2,1)} %constant.19.fh_ref, ...), custom_call_target="tpu_custom_call" | custom-call | flops 10000000000 | bytes 30000000 | tf_op jit(solution)/shard_map/pallas_call | solution.py:320
  65.5 7.3 %shard_map.140 = (bf16[256,1024]{1,0:T(8,128)(2,1)}, f32[8,3,32,512]{3,2,1,0:T(8,128)}) custom-call(bf16[256,2176]{1,0:T(8,128)(2,1)} %bitcast.20, f32[8,3,32,512]{3,2,1,0:T(8,128)} %get-tuple-element.18.xs, f32[2,512,128]{2,1,0:T(8,128)} %get-tuple-element.19.qs, f32[2,512,128]{2,1,0:T(8,128)} %get-tuple-element.20.og, f32[2,24,128]{2,1,0:T(8,128)} %bitcast.33, ...), custom_call_target="tpu_custom_call" | custom-call | flops 8000000000 | bytes 24000000 | tf_op jit(solution)/shard_map/pallas_call | solution.py:320
  72.8 14.9 %shard_map.142 = bf16[256,1024]{1,0:T(8,128)(2,1)} custom-call(f32[8,3,32,512]{3,2,1,0:T(8,128)} %get-tuple-element.24.ls, f32[8,2,32,512]{3,2,1,0:T(8,128)} %get-tuple-element.25.cs, f32[2,512,128]{2,1,0:T(8,128)} %get-tuple-element.26.ks, f32[2,512,128]{2,1,0:T(8,128)} %get-tuple-element.27.mid, f32[2,24,128]{2,1,0:T(8,128)} %bitcast.34, ...), custom_call_target="tpu_custom_call" | custom-call | flops 12000000000 | bytes 36000000 | tf_op jit(solution)/shard_map/pallas_call | solution.py:320
  87.7 18.5 %all_to_all.25 = bf16[8,32,1024]{2,1,0:T(8,128)(2,1)} all-to-all(bf16[8,32,1024]{2,1,0:T(8,128)(2,1)} %bitcast.26), channel_id=1, replica_groups=mesh['seq'=8,'chan'=4] {'seq'}, dimensions={0} | all-to-all | bytes 1048576 | tf_op jit(solution)/shard_map/all_to_all | solution.py:333
  106.1 17.6 %all_to_all.26 = bf16[8,32,1024]{2,1,0:T(8,128)(2,1)} all-to-all(bf16[8,32,1024]{2,1,0:T(8,128)(2,1)S(1)} %bitcast.22), channel_id=1, replica_groups=mesh['seq'=8,'chan'=4] {'seq'}, dimensions={0} | all-to-all | bytes 1048576 | tf_op jit(solution)/shard_map/all_to_all | solution.py:333
  123.8 3.6 %all-to-all-start.4 = ((bf16[8,32,1024]{2,1,0:T(8,128)(2,1)}), bf16[8,32,1024]{2,1,0:T(8,128)(2,1)S(1)}, u32[]{:S(2)}, u32[]{:S(2)}) async-start(bf16[8,32,1024]{2,1,0:T(8,128)(2,1)} %bitcast.13), calls=%async_computation.4 | async-start | bytes 1048576 | tf_op jit(solution)/shard_map/all_to_all | solution.py:333
  127.4 2.0 %shard_map.143 = (bf16[512,256]{1,0:T(8,128)(2,1)}, bf16[512,256]{1,0:T(8,128)(2,1)}) custom-call(bf16[256,1024]{1,0:T(8,128)(2,1)} %bitcast.25), custom_call_target="tpu_custom_call" | custom-call | flops 3000000000 | bytes 9000000 | tf_op jit(solution)/shard_map/pallas_call | solution.py:320
  129.4 2.0 %shard_map.141 = (bf16[512,256]{1,0:T(8,128)(2,1)}, bf16[512,256]{1,0:T(8,128)(2,1)}) custom-call(bf16[256,1024]{1,0:T(8,128)(2,1)} %bitcast.24), custom_call_target="tpu_custom_call" | custom-call | flops 3000000000 | bytes 9000000 | tf_op jit(solution)/shard_map/pallas_call | solution.py:320
  131.3 10.2 %all-to-all-done.4 = bf16[8,32,1024]{2,1,0:T(8,128)(2,1)S(1)} async-done(((bf16[8,32,1024]{2,1,0:T(8,128)(2,1)}), bf16[8,32,1024]{2,1,0:T(8,128)(2,1)S(1)}, u32[]{:S(2)}, u32[]{:S(2)}) %all-to-all-start.4) | async-done | bytes 524320 | tf_op jit(solution)/shard_map/all_to_all | solution.py:333
  141.5 0.8 copy-done.4
  142.3 2.0 %shard_map.144 = f32[512,256]{1,0:T(8,128)} custom-call(bf16[256,1024]{1,0:T(8,128)(2,1)} %bitcast.23), custom_call_target="tpu_custom_call" | custom-call | flops 3000000000 | bytes 9000000 | tf_op jit(solution)/shard_map/pallas_call | solution.py:320
  (17 shorter events, 0.2 us)
Async XLA Ops:
  0.6 27.6 %copy-start = (f32[128,256]{1,0:T(8,128)S(1)}, f32[128,256]{1,0:T(8,128)}, u32[]{:S(2)}) copy-start(f32[128,256]{1,0:T(8,128)} %param.14) | copy-start | bytes 393220
  2.7 21.8 %all-to-all-start.1 = ((bf16[8,32,1024]{2,1,0:T(8,128)(2,1)}), bf16[8,32,1024]{2,1,0:T(8,128)(2,1)S(1)}, u32[]{:S(2)}, u32[]{:S(2)}) async-start(bf16[8,32,1024]{2,1,0:T(8,128)(2,1)} %bitcast.27), calls=%async_computation.1 | async-start | bytes 1048576 | tf_op jit(solution)/shard_map/all_to_all | solution.py:333
  16.1 12.3 %copy-start.5 = (f32[3,7,256]{2,1,0:T(8,128)S(1)}, f32[3,7,256]{2,1,0:T(8,128)}, u32[]{:S(2)}) copy-start(f32[3,7,256]{2,1,0:T(8,128)} %param.13) | copy-start | bytes 64516
  24.5 5.5 %copy-start.2 = (bf16[8,32,1024]{2,1,0:T(8,128)(2,1)}, bf16[8,32,1024]{2,1,0:T(8,128)(2,1)S(1)}, u32[]{:S(2)}) copy-start(bf16[8,32,1024]{2,1,0:T(8,128)(2,1)S(1)} %all-to-all-done.1) | copy-start | bytes 1572868
  24.5 5.5 %copy-start.6 = (s32[1024]{0:T(1024)S(1)}, s32[1024]{0:T(1024)}, u32[]{:S(2)}) copy-start(s32[1024]{0:T(1024)} %param.18) | copy-start | bytes 12292
  24.5 31.1 %all-to-all-start = ((bf16[8,32,2176]{2,1,0:T(8,128)(2,1)}), bf16[8,32,2176]{2,1,0:T(8,128)(2,1)S(1)}, u32[]{:S(2)}, u32[]{:S(2)}) async-start(bf16[8,32,2176]{2,1,0:T(8,128)(2,1)} %bitcast.18), calls=%async_computation | async-start | bytes 2228224 | tf_op jit(solution)/shard_map/all_to_all | solution.py:333
  55.6 1.0 copy-start.1
  72.8 33.4 %copy-start.3 = (bf16[256,1024]{1,0:T(8,128)(2,1)S(1)}, bf16[256,1024]{1,0:T(8,128)(2,1)}, u32[]{:S(2)}) copy-start(bf16[256,1024]{1,0:T(8,128)(2,1)} %get-tuple-element.21) | copy-start | bytes 1572868
  123.8 17.7 %all-to-all-start.4 = ((bf16[8,32,1024]{2,1,0:T(8,128)(2,1)}), bf16[8,32,1024]{2,1,0:T(8,128)(2,1)S(1)}, u32[]{:S(2)}, u32[]{:S(2)}) async-start(bf16[8,32,1024]{2,1,0:T(8,128)(2,1)} %bitcast.13), calls=%async_computation.4 | async-start | bytes 1048576 | tf_op jit(solution)/shard_map/all_to_all | solution.py:333
  141.5 0.8 copy-start.4
